TPU v7x, 128 devices: a whole 4x4x4 slice. The times are simulated.
128 devices in a mesh: gz: 4 (over x), gx: 32 (over y, z, core).
Axes of the slice: x: 4, y: 4, z: 4, core: 2. Of those that a mesh axis runs over, the one named last changes fastest.
Arguments:
- populations: float32 [27, 8, 256, 128], P(None, 'gz', 'gx'), may hold values from 0 to 1, as said below
- rates: float32 [27], replicated, may hold values from 0.5 to 1.8
- grain_fraction: bfloat16 [65536, 128], P(('gz', 'gx')), may hold values from 0 to 0.3984375
- grain_velocity: bfloat16 [3, 65536], P(None, ('gz', 'gx')), may hold values from -0.29882812 to 0.29882812
- grain_dest: int32 [65536, 1], P(('gz', 'gx')), may hold values from 0 to 127; in each aligned block of 512 rows (0 to 511, 512 to 1023, ...) at most 8 rows name the same one
- grain_line: int32 [65536], P(('gz', 'gx')), may hold values from 0 to 15
Outputs:
- scaled: float32 [27, 8, 256, 128], P(None, 'gz', 'gx')
- grain_force: float32 [3, 65536], P(None, ('gz', 'gx'))
Inputs may be any that keep to these rules, and one draw needn't show every extreme that they name: populations are positive. grain_dest is a linear index of gz+gx, gz slowest; among the rows of one device at most 8 name the same device, and exactly 8 do in some device's rows.
All inputs are finite; a program needn't handle non-finite values.
Results may differ from a plain program's by a relative error of at most 0.0003.
Values may be sent and summed in bfloat16 or wider, within the bound.
A program may use at most 64 MiB of HBM per device.

v0:
```python
import math

import jax
import jax.numpy as jnp
import numpy as np
from jax import lax
from jax.sharding import PartitionSpec as P

STEPS = 2


highest = lax.Precision.HIGHEST


def side_by_side(arrays, axis, split_dim, concat_dim, along):
    widths = [math.prod(a.shape[along:]) for a in arrays]
    both = jnp.concatenate(
        [a.reshape(*a.shape[:along], w) for a, w in zip(arrays, widths)], axis=along
    )
    filled = lax.all_to_all(both, axis, split_axis=split_dim, concat_axis=concat_dim, tiled=True)
    parts = jnp.split(filled, [sum(widths[:k]) for k in range(1, len(widths))], axis=along)
    return tuple(
        (b.reshape(*filled.shape[:along], *a.shape[along:]) for a, b in zip(arrays, parts))
    )


def extended_2(shard, sides, width):
    for axis, dim in sides:
        peers, length = (lax.axis_size(axis), shard.shape[dim])
        up = [(i, (i + 1) % peers) for i in range(peers)]
        down = [(j, i) for i, j in up]
        last = lax.slice_in_dim(shard, length - width, length, axis=dim)
        first = lax.slice_in_dim(shard, 0, width, axis=dim)
        before = lax.ppermute(last, axis, up)
        after = lax.ppermute(first, axis, down)
        shard = jnp.concatenate([before, shard, after], axis=dim)
    return shard


def lattice_tables():
    labels = np.arange(27)
    digits = [labels // 9, labels // 3 % 3, labels % 3]
    velocity = np.stack([digit - 1 for digit in digits]).astype(np.float32)
    count = np.abs(digits[0] - 1) + np.abs(digits[1] - 1) + np.abs(digits[2] - 1)
    weights = np.array([8.0 / 27, 2.0 / 27, 1.0 / 54, 1.0 / 216], dtype=np.float32)[count]
    vander = np.array([[1.0, 1.0, 1.0], [-1.0, 0.0, 1.0], [1.0, 0.0, 1.0]], dtype=np.float32)
    vander_inv = np.array([[0.0, -0.5, 0.5], [1.0, 0.0, -1.0], [0.0, 0.5, 0.5]], dtype=np.float32)
    moments = np.ones((27, 27), dtype=np.float32)
    inverse = np.ones((27, 27), dtype=np.float32)
    for digit in digits:
        moments = moments * vander[digit[:, None], digit[None, :]]
        inverse = inverse * vander_inv[digit[:, None], digit[None, :]]
    return (velocity, weights, moments, inverse)


def equilibrium(density, speed, velocity, weights):
    along = jnp.dot(velocity.T, speed, precision=highest)
    square = jnp.sum(speed * speed, axis=0)
    return (
        weights[:, None]
        * density[None, :]
        * (1.0 + 3.0 * along + 4.5 * along * along - 1.5 * square[None, :])
    )


def collide(fields, rates, solid, carried):
    velocity_np, weights_np, moments_np, inverse_np = lattice_tables()
    velocity = jnp.asarray(velocity_np)
    weights = jnp.asarray(weights_np)
    density = jnp.sum(fields, axis=0)
    momentum = jnp.dot(velocity, fields, precision=highest)
    speed = momentum / density[None, :]
    equil = equilibrium(density, speed, velocity, weights)
    departure = fields - equil
    projected = jnp.dot(jnp.asarray(moments_np), departure, precision=highest)
    fluid = -jnp.dot(jnp.asarray(inverse_np), rates[:, None] * projected, precision=highest)
    cover = 1.0 + solid
    share = solid / cover
    solid_equil = equilibrium(density, carried / cover[None, :], velocity, weights)
    exchange_term = departure[::-1] - (fields - solid_equil)
    post = fields + (1.0 - share)[None, :] * fluid + share[None, :] * exchange_term
    push = jnp.dot(velocity, exchange_term, precision=highest) / cover[None, :]
    return (post, push)


def stream_local(block, extended, level, top):
    depth, length = (block.shape[1], block.shape[2])
    moved_list = []
    for population in range(27):
        step_z = population // 9 - 1
        step_x = population // 3 % 3 - 1
        step_y = population % 3 - 1
        moved = extended[
            population, 1 - step_z : 1 - step_z + depth, 1 - step_x : 1 - step_x + length
        ]
        moved = jnp.roll(moved, step_y, axis=2)
        if step_z == 1:
            moved = jnp.where((level == 0)[:, None, None], block[26 - population], moved)
        if step_z == -1:
            moved = jnp.where((level == top)[:, None, None], block[26 - population], moved)
        moved_list.append(moved)
    return jnp.stack(moved_list)


def per_device(populations, rates, grain_fraction, grain_velocity, grain_dest, grain_line):
    depth, length, width = (populations.shape[1], populations.shape[2], populations.shape[3])
    lines = depth * length
    cells = lines * width
    devices = lax.axis_size("gz") * lax.axis_size("gx")
    grains = grain_fraction.shape[0]
    capacity = 2 * grains // devices
    slots = devices * capacity
    target = grain_dest[:, 0]
    chosen = (target[:, None] == jnp.arange(devices, dtype=jnp.int32)[None, :]).astype(jnp.int32)
    before = jnp.cumsum(chosen, axis=0) - chosen
    rank = jnp.sum(before * chosen, axis=1)
    position = target * capacity + rank
    send_fraction = (
        jnp.zeros((slots, width), jnp.bfloat16)
        .at[position]
        .set(grain_fraction)
        .reshape(devices, capacity, width)
    )
    send_speed = (
        jnp.zeros((devices, 3, capacity), jnp.bfloat16).at[target, :, rank].set(grain_velocity.T)
    )
    send_line = (
        jnp.full((slots,), -1, jnp.int32).at[position].set(grain_line).reshape(devices, capacity)
    )
    recv_fraction, recv_speed = side_by_side((send_fraction, send_speed), ("gz", "gx"), 0, 0, 1)
    recv_line = lax.all_to_all(
        send_line, ("gz", "gx"), split_axis=0, concat_axis=0, tiled=True
    ).reshape(slots)
    fraction = recv_fraction.reshape(slots, width)
    speed = jnp.moveaxis(recv_speed, 1, 0).reshape(3, slots).astype(jnp.float32)
    matches = jnp.arange(lines, dtype=jnp.int32)[:, None] == recv_line[None, :]
    solid = jnp.dot(matches.astype(jnp.bfloat16), fraction, preferred_element_type=jnp.float32)
    weighted = fraction.astype(jnp.float32)[None, :, :] * speed[:, :, None]
    carried = jnp.einsum("ls,ksy->kly", matches.astype(jnp.float32), weighted, precision=highest)
    solid_flat = solid.reshape(cells)
    carried_flat = carried.reshape(3, cells)
    fields = populations.reshape(27, cells)
    push_total = jnp.zeros((3, cells), jnp.float32)
    level = lax.axis_index("gz") * depth + jnp.arange(depth, dtype=jnp.int32)
    top = lax.axis_size("gz") * depth - 1
    for turn_index in range(STEPS):
        post, push = collide(fields, rates, solid_flat, carried_flat)
        push_total = push_total + push
        block = post.reshape(27, depth, length, width)
        extended = extended_2(block, (("gz", 1), ("gx", 2)), 1)
        fields = stream_local(block, extended, level, top).reshape(27, cells)
    weights = jnp.asarray(lattice_tables()[1])
    scaled = fields.reshape(27, depth, length, width) / weights[:, None, None, None]
    push_lines = push_total.reshape(3, lines, width)
    safe_line = jnp.where(recv_line >= 0, recv_line, 0).reshape(devices, capacity)
    picked = push_lines[:, safe_line, :]
    slot_force = -jnp.einsum(
        "kjcy,jcy->jkc",
        picked,
        fraction.reshape(devices, capacity, width).astype(jnp.float32),
        precision=highest,
    )
    returned = lax.all_to_all(slot_force, ("gz", "gx"), split_axis=0, concat_axis=0, tiled=True)
    grain_force = returned[target, :, rank].T
    return (scaled, grain_force)


def solution(mesh):
    in_specs = (
        P(None, "gz", "gx", None),
        P(),
        P(("gz", "gx"), None),
        P(None, ("gz", "gx")),
        P(("gz", "gx"), None),
        P(("gz", "gx")),
    )
    out_specs = (P(None, "gz", "gx", None), P(None, ("gz", "gx")))
    return jax.shard_map(
        per_device, mesh=mesh, in_specs=in_specs, out_specs=out_specs, check_vma=False
    )
```

profile of v0, /device:TPU:0, one launch (start us, length us, event | category | flops | bytes accessed | tf_op | source)
XLA Modules:
  0.0 138.7 jit_solution(3843627713270048757)
XLA Ops:
  0.6 0.8 copy.182
  1.8 0.9 fusion.27
  2.7 0.7 or_select_fusion
  3.4 2.6 %scatter_custom_fusion = s32[1024]{0:T(1024)S(1)} fusion(s32[512]{0:T(512)S(1)} %bitcast.564, s32[512]{0:T(512)} %param.20, s32[]{:T(128)} %constant.25.clone.1), kind=kCustom, calls=%fused_computation.312 | custom fusion | bytes 4608 | tf_op jit(solution)/shard_map/scatter | solution.py:128
  6.0 0.7 all_to_all.19
  6.7 11.2 %all-to-all-start = ((s32[128,1,8]{2,1,0:T(1,128)}), s32[128,1,8]{2,1,0:T(1,128)S(1)}, u32[]{:S(2)}, u32[]{:S(2)}) async-start(s32[128,1,8]{2,1,0:T(1,128)} %bitcast.8), calls=%async_computation | async-start | bytes 131072 | tf_op jit(solution)/shard_map/all_to_all | solution.py:131
  17.9 0.9 copy.185
  18.8 2.2 %scatter_custom_fusion.1 = bf16[1024,128]{1,0:T(8,128)(2,1)S(1)} fusion(s32[512]{0:T(512)S(1)} %bitcast.565, bf16[512,128]{1,0:T(8,128)(2,1)} %param.17, bf16[]{:T(256)} %constant.11.clone.1), kind=kCustom, calls=%fused_computation.58 | custom fusion | bytes 262656 | tf_op jit(solution)/shard_map/scatter | solution.py:121
  21.8 23.3 %scatter_fusion = bf16[128,3,8]{1,2,0:T(8,128)(2,1)S(1)} fusion(bf16[128,3,8]{1,2,0:T(8,128)(2,1)S(1)} %broadcast_in_dim.211, s32[512]{0:T(512)S(1)} %bitcast.426, bf16[512,3]{1,0:T(8,128)(2,1)S(1)} %copy.185), kind=kCustom, calls=%fused_computation.4 | custom fusion | bytes 13312 | tf_op jit(solution)/shard_map/scatter | solution.py:125
  45.4 0.5 fusion.14
  46.3 0.4 rev.6
  46.9 0.5 broadcast.575
  47.5 0.8 reduce.36
  48.5 1.1 reshape.983
  49.6 9.7 %all-to-all-start.1 = ((bf16[128,2,524]{2,1,0:T(2,128)(2,1)}), bf16[128,2,524]{2,1,0:T(2,128)(2,1)S(1)}, u32[]{:S(2)}, u32[]{:S(2)}) async-start(bf16[128,2,524]{2,1,0:T(2,128)(2,1)} %reshape.983), calls=%async_computation.1 | async-start | bytes 655360 | tf_op jit(solution)/shard_map/all_to_all | solution.py:20
  59.3 0.5 broadcast.517
  59.8 0.8 reduce.35
  60.9 10.1 %all-to-all-done.1 = bf16[128,2,524]{2,1,0:T(2,128)(2,1)S(1)} async-done(((bf16[128,2,524]{2,1,0:T(2,128)(2,1)}), bf16[128,2,524]{2,1,0:T(2,128)(2,1)S(1)}, u32[]{:S(2)}, u32[]{:S(2)}) %all-to-all-start.1) | async-done | bytes 268320 | tf_op jit(solution)/shard_map/all_to_all | solution.py:20
  70.9 0.5 reshape.984
  71.5 0.9 copy.189
  73.2 0.8 fusion.45
  74.0 0.5 fusion.23
  74.5 0.4 fusion.3
  75.0 0.6 collective-permute-start
  75.7 0.4 convolution_divide_fusion.1
  76.0 2.7 %collective-permute-start.1 = (f32[27,1,8,128]{3,2,1,0:T(8,128)S(1)}, f32[27,1,8,128]{3,2,1,0:T(8,128)S(1)}, u32[]{:S(2)}, u32[]{:S(2)}) collective-permute-start(f32[27,1,8,128]{3,2,1,0:T(8,128)S(1)} %get-tuple-element.135), channel_id=1, source_target_pairs={{32,0},{64,32},{96,64},{0,96},{33,1},{65,33},{97,65},{1,97},{34,2}... | collective-permute-start | bytes 331784 | tf_op jit(solution)/shard_map/ppermute | solution.py:35
  79.0 2.1 %collective-permute-done = f32[27,1,8,128]{3,2,1,0:T(8,128)S(1)} collective-permute-done((f32[27,1,8,128]{3,2,1,0:T(8,128)S(1)}, f32[27,1,8,128]{3,2,1,0:T(8,128)S(1)}, u32[]{:S(2)}, u32[]{:S(2)}) %collective-permute-start) | collective-permute-done | bytes 110624 | tf_op jit(solution)/shard_map/ppermute | solution.py:34
  82.1 5.1 %collective-permute-start.2 = (f32[27,4,1,128]{3,2,1,0:T(1,128)S(1)}, f32[27,4,1,128]{3,2,1,0:T(1,128)S(1)}, u32[]{:S(2)}, u32[]{:S(2)}) collective-permute-start(f32[27,4,1,128]{3,2,1,0:T(1,128)S(1)} %get-tuple-element.64), channel_id=1, source_target_pairs={{1,0},{2,1},{3,2},{4,3},{5,4},{6,5},{7,6},{8,7},{9,8},{10,9},{11,1... | collective-permute-start | bytes 165896 | tf_op jit(solution)/shard_map/ppermute | solution.py:35
  87.5 1.5 %collective-permute-done.3 = f32[27,4,1,128]{3,2,1,0:T(1,128)S(1)} collective-permute-done((f32[27,4,1,128]{3,2,1,0:T(1,128)S(1)}, f32[27,4,1,128]{3,2,1,0:T(1,128)S(1)}, u32[]{:S(2)}, u32[]{:S(2)}) %collective-permute-start.3) | collective-permute-done | bytes 55328 | tf_op jit(solution)/shard_map/ppermute | solution.py:34
  91.5 0.4 stack.114
  91.8 0.5 fusion.17
  92.4 0.4 rev.7
  93.2 0.4 fusion.11
  93.6 0.4 fusion.7
  94.0 0.7 fusion.62
  94.9 3.5 %gather_fusion = f32[1024,3,128]{2,1,0:T(4,128)S(1)} fusion(f32[3,16,128]{2,0,1:T(4,128)S(1)} %fusion.11, s32[1024]{0:T(1024)S(1)} %broadcast_clamp_fusion), kind=kCustom, calls=%fused_computation | custom fusion | bytes 3149824 | tf_op jit(solution)/shard_map/gather | solution.py:156
  98.4 1.2 multiply_reduce_fusion
  99.7 1.5 %copy.231 = f32[128,8,3]{1,2,0:T(4,128)} copy(f32[128,8,3]{2,1,0:T(8,128)S(1)} %neg.18) | data formatting | bytes 24576
  101.2 10.9 %all-to-all-start.2 = ((f32[128,3,8]{2,1,0:T(4,128)}), f32[128,3,8]{2,1,0:T(4,128)S(1)}, u32[]{:S(2)}, u32[]{:S(2)}) async-start(f32[128,3,8]{2,1,0:T(4,128)} %bitcast.199), calls=%async_computation.2 | async-start | bytes 524288 | tf_op jit(solution)/shard_map/all_to_all | solution.py:163
  112.2 2.2 %collective-permute-start.5 = (f32[27,1,8,128]{3,2,1,0:T(8,128)S(1)}, f32[27,1,8,128]{3,2,1,0:T(8,128)S(1)}, u32[]{:S(2)}, u32[]{:S(2)}) collective-permute-start(f32[27,1,8,128]{3,2,1,0:T(8,128)S(1)} %get-tuple-element.133), channel_id=1, source_target_pairs={{32,0},{64,32},{96,64},{0,96},{33,1},{65,33},{97,65},{1,97},{34,2}... | collective-permute-start | bytes 331784 | tf_op jit(solution)/shard_map/ppermute | solution.py:35
  114.4 8.6 %all-to-all-done.2 = f32[128,3,8]{2,1,0:T(4,128)S(1)} async-done(((f32[128,3,8]{2,1,0:T(4,128)}), f32[128,3,8]{2,1,0:T(4,128)S(1)}, u32[]{:S(2)}, u32[]{:S(2)}) %all-to-all-start.2) | async-done | bytes 12320 | tf_op jit(solution)/shard_map/all_to_all | solution.py:163
  123.0 0.8 copy.217
  123.8 2.6 %gather_fusion.1 = f32[512,3]{1,0:T(8,128)S(1)} fusion(f32[128,3,8]{1,2,0:T(8,128)S(1)} %copy.217, s32[512]{0:T(512)S(1)} %bitcast.425), kind=kCustom, calls=%fused_computation.1 | custom fusion | bytes 16384 | tf_op jit(solution)/shard_map/gather | solution.py:164
  126.5 0.7 copy.218
  127.6 0.5 collective-permute-start.6
  128.2 1.7 %collective-permute-done.6 = f32[27,4,1,128]{3,2,1,0:T(1,128)S(1)} collective-permute-done((f32[27,4,1,128]{3,2,1,0:T(1,128)S(1)}, f32[27,4,1,128]{3,2,1,0:T(1,128)S(1)}, u32[]{:S(2)}, u32[]{:S(2)}) %collective-permute-start.6) | collective-permute-done | bytes 55328 | tf_op jit(solution)/shard_map/ppermute | solution.py:35
  130.1 5.0 %collective-permute-done.7 = f32[27,4,1,128]{3,2,1,0:T(1,128)S(1)} collective-permute-done((f32[27,4,1,128]{3,2,1,0:T(1,128)S(1)}, f32[27,4,1,128]{3,2,1,0:T(1,128)S(1)}, u32[]{:S(2)}, u32[]{:S(2)}) %collective-permute-start.7) | collective-permute-done | bytes 55328 | tf_op jit(solution)/shard_map/ppermute | solution.py:34
  137.9 0.8 broadcast_multiply_fusion
  (259 shorter events, 10.7 us)
Async XLA Ops:
  0.6 20.7 %copy-start = (f32[27,2,8,128]{3,2,1,0:T(8,128)S(1)}, f32[27,2,8,128]{3,2,1,0:T(8,128)}, u32[]{:S(2)}) copy-start(f32[27,2,8,128]{3,2,1,0:T(8,128)} %param.15) | copy-start | bytes 663556
  1.7 19.8 %copy-start.19 = (f32[3,27]{1,0:T(4,128)S(1)}, f32[3,27]{1,0:T(4,128)}, u32[]{:S(2)}) copy-start(f32[3,27]{1,0:T(4,128)} %constant.18.clone) | copy-start | bytes 976
  6.7 42.8 %all-to-all-start = ((s32[128,1,8]{2,1,0:T(1,128)}), s32[128,1,8]{2,1,0:T(1,128)S(1)}, u32[]{:S(2)}, u32[]{:S(2)}) async-start(s32[128,1,8]{2,1,0:T(1,128)} %bitcast.8), calls=%async_computation | async-start | bytes 131072 | tf_op jit(solution)/shard_map/all_to_all | solution.py:131
  18.8 26.6 %copy-start.20 = (f32[27]{0:T(128)S(1)}, f32[27]{0:T(128)}, u32[]{:S(2)}) copy-start(f32[27]{0:T(128)} %constant.19.clone) | copy-start | bytes 328
  21.1 24.8 %copy-start.2 = (f32[27,27]{1,0:T(8,128)S(1)}, f32[27,27]{1,0:T(8,128)}, u32[]{:S(2)}) copy-start(f32[27,27]{1,0:T(8,128)} %constant.54.clone) | copy-start | bytes 8752
  21.1 24.8 %copy-start.21 = (f32[27]{0:T(128)S(1)}, f32[27]{0:T(128)}, u32[]{:S(2)}) copy-start(f32[27]{0:T(128)} %param.16) | copy-start | bytes 328
  49.6 21.4 %all-to-all-start.1 = ((bf16[128,2,524]{2,1,0:T(2,128)(2,1)}), bf16[128,2,524]{2,1,0:T(2,128)(2,1)S(1)}, u32[]{:S(2)}, u32[]{:S(2)}) async-start(bf16[128,2,524]{2,1,0:T(2,128)(2,1)} %reshape.983), calls=%async_computation.1 | async-start | bytes 655360 | tf_op jit(solution)/shard_map/all_to_all | solution.py:20
  75.0 6.0 %collective-permute-start = (f32[27,1,8,128]{3,2,1,0:T(8,128)S(1)}, f32[27,1,8,128]{3,2,1,0:T(8,128)S(1)}, u32[]{:S(2)}, u32[]{:S(2)}) collective-permute-start(f32[27,1,8,128]{3,2,1,0:T(8,128)S(1)} %get-tuple-element.136), channel_id=1, source_target_pairs={{0,32},{32,64},{64,96},{96,0},{1,33},{33,65},{65,97},{97,1},{2,34}... | collective-permute-start | bytes 331784 | tf_op jit(solution)/shard_map/ppermute | solution.py:34
  76.0 5.1 %collective-permute-start.1 = (f32[27,1,8,128]{3,2,1,0:T(8,128)S(1)}, f32[27,1,8,128]{3,2,1,0:T(8,128)S(1)}, u32[]{:S(2)}, u32[]{:S(2)}) collective-permute-start(f32[27,1,8,128]{3,2,1,0:T(8,128)S(1)} %get-tuple-element.135), channel_id=1, source_target_pairs={{32,0},{64,32},{96,64},{0,96},{33,1},{65,33},{97,65},{1,97},{34,2}... | collective-permute-start | bytes 331784 | tf_op jit(solution)/shard_map/ppermute | solution.py:35
  81.1 9.9 %copy-start.22 = (f32[3]{0:T(128)S(1)}, f32[3]{0:T(128)}, u32[]{:S(2)}) copy-start(f32[3]{0:T(128)} %constant.109) | copy-start | bytes 40
  81.1 9.8 %copy-start.23 = (f32[3]{0:T(128)S(1)}, f32[3]{0:T(128)}, u32[]{:S(2)}) copy-start(f32[3]{0:T(128)} %constant.107) | copy-start | bytes 40
  81.1 9.8 %copy-start.24 = (f32[3]{0:T(128)S(1)}, f32[3]{0:T(128)}, u32[]{:S(2)}) copy-start(f32[3]{0:T(128)} %constant.105) | copy-start | bytes 40
  81.2 9.8 %copy-start.25 = (f32[3]{0:T(128)S(1)}, f32[3]{0:T(128)}, u32[]{:S(2)}) copy-start(f32[3]{0:T(128)} %constant.103) | copy-start | bytes 40
  81.2 9.8 %copy-start.26 = (f32[3]{0:T(128)S(1)}, f32[3]{0:T(128)}, u32[]{:S(2)}) copy-start(f32[3]{0:T(128)} %constant.101) | copy-start | bytes 40
  81.2 9.8 %copy-start.27 = (f32[3]{0:T(128)S(1)}, f32[3]{0:T(128)}, u32[]{:S(2)}) copy-start(f32[3]{0:T(128)} %constant.99) | copy-start | bytes 40
  81.2 9.8 %copy-start.28 = (f32[3]{0:T(128)S(1)}, f32[3]{0:T(128)}, u32[]{:S(2)}) copy-start(f32[3]{0:T(128)} %constant.97) | copy-start | bytes 40
  81.2 9.8 %copy-start.29 = (f32[3]{0:T(128)S(1)}, f32[3]{0:T(128)}, u32[]{:S(2)}) copy-start(f32[3]{0:T(128)} %constant.95) | copy-start | bytes 40
  81.2 9.8 %copy-start.30 = (f32[3]{0:T(128)S(1)}, f32[3]{0:T(128)}, u32[]{:S(2)}) copy-start(f32[3]{0:T(128)} %constant.93) | copy-start | bytes 40
  81.2 9.8 %copy-start.31 = (f32[3]{0:T(128)S(1)}, f32[3]{0:T(128)}, u32[]{:S(2)}) copy-start(f32[3]{0:T(128)} %constant.91) | copy-start | bytes 40
  81.2 9.8 %copy-start.32 = (f32[3]{0:T(128)S(1)}, f32[3]{0:T(128)}, u32[]{:S(2)}) copy-start(f32[3]{0:T(128)} %constant.89) | copy-start | bytes 40
  81.3 9.8 %copy-start.33 = (f32[3]{0:T(128)S(1)}, f32[3]{0:T(128)}, u32[]{:S(2)}) copy-start(f32[3]{0:T(128)} %constant.87) | copy-start | bytes 40
  81.3 9.8 %copy-start.34 = (f32[3]{0:T(128)S(1)}, f32[3]{0:T(128)}, u32[]{:S(2)}) copy-start(f32[3]{0:T(128)} %constant.83) | copy-start | bytes 40
  81.3 9.8 %copy-start.35 = (f32[3]{0:T(128)S(1)}, f32[3]{0:T(128)}, u32[]{:S(2)}) copy-start(f32[3]{0:T(128)} %constant.81) | copy-start | bytes 40
  81.3 9.8 %copy-start.36 = (f32[3]{0:T(128)S(1)}, f32[3]{0:T(128)}, u32[]{:S(2)}) copy-start(f32[3]{0:T(128)} %constant.79) | copy-start | bytes 40
  81.3 9.8 %copy-start.37 = (f32[3]{0:T(128)S(1)}, f32[3]{0:T(128)}, u32[]{:S(2)}) copy-start(f32[3]{0:T(128)} %constant.77) | copy-start | bytes 40
  81.3 9.8 %copy-start.38 = (f32[3]{0:T(128)S(1)}, f32[3]{0:T(128)}, u32[]{:S(2)}) copy-start(f32[3]{0:T(128)} %constant.75) | copy-start | bytes 40
  81.3 9.8 %copy-start.39 = (f32[3]{0:T(128)S(1)}, f32[3]{0:T(128)}, u32[]{:S(2)}) copy-start(f32[3]{0:T(128)} %constant.73) | copy-start | bytes 40
  81.3 9.8 %copy-start.40 = (f32[3]{0:T(128)S(1)}, f32[3]{0:T(128)}, u32[]{:S(2)}) copy-start(f32[3]{0:T(128)} %constant.71) | copy-start | bytes 40
  81.4 9.8 %copy-start.41 = (f32[3]{0:T(128)S(1)}, f32[3]{0:T(128)}, u32[]{:S(2)}) copy-start(f32[3]{0:T(128)} %constant.69) | copy-start | bytes 40
  81.4 9.8 %copy-start.42 = (f32[3]{0:T(128)S(1)}, f32[3]{0:T(128)}, u32[]{:S(2)}) copy-start(f32[3]{0:T(128)} %constant.67) | copy-start | bytes 40
  81.4 9.8 %copy-start.43 = (f32[3]{0:T(128)S(1)}, f32[3]{0:T(128)}, u32[]{:S(2)}) copy-start(f32[3]{0:T(128)} %constant.65) | copy-start | bytes 40
  81.4 9.8 %copy-start.44 = (f32[3]{0:T(128)S(1)}, f32[3]{0:T(128)}, u32[]{:S(2)}) copy-start(f32[3]{0:T(128)} %constant.63) | copy-start | bytes 40
  81.4 9.8 %copy-start.45 = (f32[3]{0:T(128)S(1)}, f32[3]{0:T(128)}, u32[]{:S(2)}) copy-start(f32[3]{0:T(128)} %constant.61) | copy-start | bytes 40
  81.8 7.2 %collective-permute-start.3 = (f32[27,4,1,128]{3,2,1,0:T(1,128)S(1)}, f32[27,4,1,128]{3,2,1,0:T(1,128)S(1)}, u32[]{:S(2)}, u32[]{:S(2)}) collective-permute-start(f32[27,4,1,128]{3,2,1,0:T(1,128)S(1)} %get-tuple-element.63), channel_id=1, source_target_pairs={{0,1},{1,2},{2,3},{3,4},{4,5},{5,6},{6,7},{7,8},{8,9},{9,10},{10,1... | collective-permute-start | bytes 165896 | tf_op jit(solution)/shard_map/ppermute | solution.py:34
  82.1 7.2 %collective-permute-start.2 = (f32[27,4,1,128]{3,2,1,0:T(1,128)S(1)}, f32[27,4,1,128]{3,2,1,0:T(1,128)S(1)}, u32[]{:S(2)}, u32[]{:S(2)}) collective-permute-start(f32[27,4,1,128]{3,2,1,0:T(1,128)S(1)} %get-tuple-element.64), channel_id=1, source_target_pairs={{1,0},{2,1},{3,2},{4,3},{5,4},{6,5},{7,6},{8,7},{9,8},{10,9},{11,1... | collective-permute-start | bytes 165896 | tf_op jit(solution)/shard_map/ppermute | solution.py:35
  94.8 32.4 %collective-permute-start.4 = (f32[27,1,8,128]{3,2,1,0:T(8,128)S(1)}, f32[27,1,8,128]{3,2,1,0:T(8,128)S(1)}, u32[]{:S(2)}, u32[]{:S(2)}) collective-permute-start(f32[27,1,8,128]{3,2,1,0:T(8,128)S(1)} %get-tuple-element.134), channel_id=1, source_target_pairs={{0,32},{32,64},{64,96},{96,0},{1,33},{33,65},{65,97},{97,1},{2,34}... | collective-permute-start | bytes 331784 | tf_op jit(solution)/shard_map/ppermute | solution.py:34
  101.2 21.8 %all-to-all-start.2 = ((f32[128,3,8]{2,1,0:T(4,128)}), f32[128,3,8]{2,1,0:T(4,128)S(1)}, u32[]{:S(2)}, u32[]{:S(2)}) async-start(f32[128,3,8]{2,1,0:T(4,128)} %bitcast.199), calls=%async_computation.2 | async-start | bytes 524288 | tf_op jit(solution)/shard_map/all_to_all | solution.py:163
  112.2 15.2 %collective-permute-start.5 = (f32[27,1,8,128]{3,2,1,0:T(8,128)S(1)}, f32[27,1,8,128]{3,2,1,0:T(8,128)S(1)}, u32[]{:S(2)}, u32[]{:S(2)}) collective-permute-start(f32[27,1,8,128]{3,2,1,0:T(8,128)S(1)} %get-tuple-element.133), channel_id=1, source_target_pairs={{32,0},{64,32},{96,64},{0,96},{33,1},{65,33},{97,65},{1,97},{34,2}... | collective-permute-start | bytes 331784 | tf_op jit(solution)/shard_map/ppermute | solution.py:35
  126.5 9.5 %copy-start.13 = (f32[1,2048]{1,0:T(1,128)S(1)}, f32[1,2048]{1,0:T(1,128)}, u32[]{:S(2)}) copy-start(f32[1,2048]{1,0:T(1,128)} %get-tuple-element.97) | copy-start | bytes 24580
  127.3 9.8 %copy-start.12 = (f32[1,2048]{1,0:T(1,128)S(1)}, f32[1,2048]{1,0:T(1,128)}, u32[]{:S(2)}) copy-start(f32[1,2048]{1,0:T(1,128)} %get-tuple-element.93) | copy-start | bytes 24580
  127.3 9.9 %copy-start.3 = (f32[1,2048]{1,0:T(1,128)S(1)}, f32[1,2048]{1,0:T(1,128)}, u32[]{:S(2)}) copy-start(f32[1,2048]{1,0:T(1,128)} %get-tuple-element.92) | copy-start | bytes 24580
  127.5 9.8 %copy-start.11 = (f32[1,2048]{1,0:T(1,128)S(1)}, f32[1,2048]{1,0:T(1,128)}, u32[]{:S(2)}) copy-start(f32[1,2048]{1,0:T(1,128)} %get-tuple-element.91) | copy-start | bytes 24580
  127.5 9.8 %copy-start.10 = (f32[1,2048]{1,0:T(1,128)S(1)}, f32[1,2048]{1,0:T(1,128)}, u32[]{:S(2)}) copy-start(f32[1,2048]{1,0:T(1,128)} %get-tuple-element.90) | copy-start | bytes 24580
  127.6 9.9 %copy-start.9 = (f32[1,2048]{1,0:T(1,128)S(1)}, f32[1,2048]{1,0:T(1,128)}, u32[]{:S(2)}) copy-start(f32[1,2048]{1,0:T(1,128)} %get-tuple-element.89) | copy-start | bytes 24580
  127.6 2.4 %collective-permute-start.6 = (f32[27,4,1,128]{3,2,1,0:T(1,128)S(1)}, f32[27,4,1,128]{3,2,1,0:T(1,128)S(1)}, u32[]{:S(2)}, u32[]{:S(2)}) collective-permute-start(f32[27,4,1,128]{3,2,1,0:T(1,128)S(1)} %get-tuple-element.62), channel_id=1, source_target_pairs={{1,0},{2,1},{3,2},{4,3},{5,4},{6,5},{7,6},{8,7},{9,8},{10,9},{11,1... | collective-permute-start | bytes 165896 | tf_op jit(solution)/shard_map/ppermute | solution.py:35
  128.2 9.4 %copy-start.8 = (f32[1,2048]{1,0:T(1,128)S(1)}, f32[1,2048]{1,0:T(1,128)}, u32[]{:S(2)}) copy-start(f32[1,2048]{1,0:T(1,128)} %get-tuple-element.88) | copy-start | bytes 24580
  128.2 9.5 %copy-start.7 = (f32[1,2048]{1,0:T(1,128)S(1)}, f32[1,2048]{1,0:T(1,128)}, u32[]{:S(2)}) copy-start(f32[1,2048]{1,0:T(1,128)} %get-tuple-element.87) | copy-start | bytes 24580
  128.2 6.9 %collective-permute-start.7 = (f32[27,4,1,128]{3,2,1,0:T(1,128)S(1)}, f32[27,4,1,128]{3,2,1,0:T(1,128)S(1)}, u32[]{:S(2)}, u32[]{:S(2)}) collective-permute-start(f32[27,4,1,128]{3,2,1,0:T(1,128)S(1)} %get-tuple-element.61), channel_id=1, source_target_pairs={{0,1},{1,2},{2,3},{3,4},{4,5},{5,6},{6,7},{7,8},{8,9},{9,10},{10,1... | collective-permute-start | bytes 165896 | tf_op jit(solution)/shard_map/ppermute | solution.py:34
  (10 other events, 71.5 us)
where the time goes:
time: 139 us
  local copies, waits for them, and re-layouts  50.7 us (36%)
  starting transfers between devices  43.3 us (31%)
  waiting for transfers between devices  29 us (21%)
  other arithmetic  8.97 us (6%)
  matrix products  4.94 us (4%)
  between operations  1.9 us (1%)
    scatter x2, local copies, waits for them, and re-layouts, per_device(): jnp.zeros((devices, 3, capacity), jnp.bfloat16).at[target, :, rank]  23.5 us
    all_to_all x1, starting transfers between devices, per_device(): lax.all_to_all(send_line, ('gz', 'gx'), split_axis=0, concat_axis=0, tile...  11.2 us
    all_to_all x1, starting transfers between devices, per_device(): lax.all_to_all(slot_force, ('gz', 'gx'), split_axis=0, concat_axis=0, til...  10.9 us
    ppermute x4, starting transfers between devices, extended_2(): after = lax.ppermute(first, axis, down)  10.5 us
    all_to_all x1, waiting for transfers between devices, side_by_side(): lax.all_to_all(both, axis, split_axis=split_dim, concat_axis=concat_dim,...  10.1 us
    all_to_all x1, starting transfers between devices, side_by_side(): lax.all_to_all(both, axis, split_axis=split_dim, concat_axis=concat_dim,...  9.72 us
    ppermute x4, waiting for transfers between devices, extended_2(): before = lax.ppermute(last, axis, up)  8.62 us
    all_to_all x1, waiting for transfers between devices, per_device(): lax.all_to_all(slot_force, ('gz', 'gx'), split_axis=0, concat_axis=0, til...  8.58 us
  transfers between devices with their start and end apart: 11, of which 6 were waited for; matrix products, arithmetic and copies ran while one was open for 33% of the time, Pallas kernels for 0%

commit v1 on v0

v1 whole, which is shorter than its diff:
```python
import functools
import itertools

import jax
import jax.numpy as jnp
import numpy as np
from jax import lax
from jax.experimental import pallas as pl
from jax.experimental.pallas import tpu as pltpu
from jax.sharding import PartitionSpec as P

MESH = pl.DeviceIdType.MESH
F32 = jnp.float32
BF16 = jnp.bfloat16
DEV = 128
CAP = 8
GRAINS = 512
SLOTS = DEV * CAP
VEL = [(i // 9 - 1, i // 3 % 3 - 1, i % 3 - 1) for i in range(27)]
WEIGHT = [(8.0 / 27, 2.0 / 27, 1.0 / 54, 1.0 / 216)[sum(map(abs, c))] for c in VEL]
NT = (((1,), (1,)), ((), ()))


def ring(v):
    return min(v, 4 - v)


OFFSETS = sorted(
    (o for o in itertools.product(range(4), range(4), range(4), range(2)) if any(o)),
    key=lambda o: -(ring(o[0]) + ring(o[1]) + ring(o[2]) + 0.3 * o[3]),
)


def iota(shape, dim, dtype=jnp.int32):
    out = lax.broadcasted_iota(jnp.int32, shape, dim)
    return out if dtype == jnp.int32 else out.astype(dtype)


def one_hot(mask):
    return jnp.where(mask, 1.0, 0.0).astype(BF16)


def split(x):
    high = x.astype(BF16)
    low = (x - high.astype(F32)).astype(BF16)
    return high, low


def nt(a, b):
    return lax.dot_general(a, b, NT, preferred_element_type=F32)


def nn(a, b):
    return jnp.dot(a, b, preferred_element_type=F32)


def along_axes(values, triple):
    for stride in (1, 3, 9):
        out = [None] * 27
        for base in range(27):
            if base // stride % 3 == 0:
                idx = (base, base + stride, base + 2 * stride)
                for k, v in zip(idx, triple(*(values[j] for j in idx))):
                    out[k] = v
        values = out
    return values


def to_moments(a, b, c):
    s = a + c
    return s + b, c - a, s


def from_moments(m0, m1, m2):
    h0, h1 = 0.5 * m2, 0.5 * m1
    return h0 - h1, m0 - m2, h0 + h1


def moments(f):
    plane = {}
    rho = None
    mom = [None, None, None]
    for i in range(27):
        rho = f[i] if rho is None else rho + f[i]
        for k in range(3):
            if VEL[i][k]:
                key = (k, VEL[i][k])
                plane[key] = f[i] if key not in plane else plane[key] + f[i]
    for k in range(3):
        mom[k] = plane[(k, 1)] - plane[(k, -1)]
    return rho, mom


def equilibrium(rho, v):
    t = [3.0 * q for q in v]
    base = rho * (1.0 - 1.5 * (v[0] * v[0] + v[1] * v[1] + v[2] * v[2]))
    half = 0.5 * rho
    out = [None] * 27
    for i in range(13):
        along = None
        c = VEL[26 - i]
        for k in range(3):
            if c[k]:
                term = t[k]
                if along is None:
                    along = term if c[k] > 0 else -term
                else:
                    along = along + term if c[k] > 0 else along - term
        even = base + half * (along * along)
        odd = rho * along
        out[26 - i] = WEIGHT[i] * (even + odd)
        out[i] = WEIGHT[i] * (even - odd)
    out[13] = WEIGHT[13] * base
    return out


def kernel(
    pop_in, rates, frac_in, vel_in, dest_in, line_in,
    f_out, force_out,
    pop, frac, vel, dest, line,
    send_f, send_m, recv_f, recv_m, send_r, recv_r,
    keep, mix, post, edge_s, corner_s, edge_r, corner_r, z_r,
    chosen_s, rank_s, match_s, cells,
    in_sem, a_send, a_recv, h_send, h_recv, own_sem,
):
    gz, gx = lax.axis_index("gz"), lax.axis_index("gx")
    me = gz * 32 + gx
    yy, zz, core = gx // 8, gx // 2 % 4, gx % 2

    def peer(o):
        x = lax.rem(gz + o[0], 4)
        rest = lax.rem(yy + o[1], 4) * 8 + lax.rem(zz + o[2], 4) * 2 + lax.rem(core + o[3], 2)
        return x, rest

    barrier = pltpu.get_barrier_semaphore()
    for o in OFFSETS:
        pl.semaphore_signal(barrier, inc=1, device_id=peer(o), device_id_type=MESH)

    loads = [
        pltpu.make_async_copy(src, dst, in_sem.at[k])
        for k, (src, dst) in enumerate(
            ((dest_in, dest), (line_in, line), (vel_in, vel), (frac_in, frac), (pop_in, pop))
        )
    ]
    for load in loads:
        load.start()

    earlier = one_hot(iota((GRAINS, GRAINS), 0) < iota((GRAINS, GRAINS), 1))
    loads[0].wait()
    target = dest[...]
    chosen = iota((DEV, GRAINS), 0) == target
    chosen_b = one_hot(chosen)
    chosen_s[...] = chosen_b
    before = nn(chosen_b, earlier)
    rank = jnp.sum(jnp.where(chosen, before, 0.0), axis=0, keepdims=True)
    rank_mask = jnp.where(iota((CAP, GRAINS), 0, F32) == rank, 1.0, 0.0)
    rank_s[...] = rank_mask

    loads[1].wait()
    loads[2].wait()
    speed = vel[...].astype(F32)
    values = [line[...].astype(F32)] + [speed[k : k + 1] for k in range(3)]
    rows = [rank_mask * v for v in values] + [jnp.zeros((DEV - 4 * CAP, GRAINS), F32)]
    send_m[...] = nt(chosen_b, jnp.concatenate(rows, axis=0).astype(BF16)).reshape(DEV, 1, 128)

    loads[3].wait()
    place = target.astype(F32) * CAP + rank
    fractions = frac[...]
    for j in range(8):
        pick = one_hot(iota((128, GRAINS), 0, F32) + 128.0 * j == place)
        send_f[16 * j : 16 * j + 16] = nn(pick, fractions).astype(BF16).reshape(16, CAP, 128)

    pl.semaphore_wait(barrier, DEV - 1)

    def to_all(src, dst, k):
        for o in OFFSETS:
            d = peer(o)
            pltpu.make_async_remote_copy(
                src_ref=src.at[d[0] * 32 + d[1]],
                dst_ref=dst.at[me],
                send_sem=a_send.at[k],
                recv_sem=a_recv.at[k],
                device_id=d,
                device_id_type=MESH,
            ).start()

    def wait_all(src, dst, sem):
        pltpu.make_async_copy(src.at[pl.ds(0, DEV - 1)], dst.at[pl.ds(0, DEV - 1)], sem).wait()

    to_all(send_m, recv_m, 0)
    to_all(send_f, recv_f, 1)
    own = [
        pltpu.make_async_copy(send_m.at[me], recv_m.at[me], own_sem.at[0]),
        pltpu.make_async_copy(send_f.at[me], recv_f.at[me], own_sem.at[1]),
    ]
    for copy in own:
        copy.start()

    def relax(f, departure, level):
        projected = along_axes(departure, to_moments)
        scaled = [projected[a] * (-rates[a]) for a in range(27)]
        return along_axes(scaled, from_moments)

    def collide(f, rho, mom, level):
        inverse = 1.0 / rho
        equil = equilibrium(rho, [m * inverse for m in mom])
        departure = [f[i] - equil[i] for i in range(27)]
        fluid = relax(f, departure, level)
        for i in range(27):
            keep[i, level] = f[i] + fluid[i]
            mix[i, level] = departure[26 - i] - f[i] - fluid[i]

    def finish(step, level, rho, share, us):
        equil = equilibrium(rho, us)
        for i in range(27):
            post[step, i, level] = keep[i, level] + share * (mix[i, level] + equil[i])

    loads[4].wait()
    first = []
    for level in range(2):
        f = [pop[i, level] for i in range(27)]
        rho, mom = moments(f)
        first.append((rho, mom))
        collide(f, rho, mom, level)

    wait_all(send_m, recv_m, a_recv.at[0])
    own[0].wait()
    diag = iota((CAP, 128), 0) == iota((CAP, 128), 1) % CAP
    spread = jnp.concatenate(
        [jnp.where(diag, jnp.broadcast_to(recv_m[s], (CAP, 128)), 0.0) for s in range(DEV)], axis=0
    ).astype(BF16)
    sel = one_hot(iota((CAP, 128), 0) == iota((CAP, 128), 1) // CAP)
    info = nt(sel, spread)
    match = jnp.where(iota((16, SLOTS), 0, F32) == info[0:1], 1.0, 0.0)
    match_s[...] = match
    weights = jnp.concatenate(
        [match] + [match * info[k : k + 1] for k in range(1, 4)], axis=0
    ).astype(BF16)

    wait_all(send_f, recv_f, a_recv.at[1])
    own[1].wait()
    summed = nn(weights, recv_f[...].reshape(SLOTS, 128))
    covers = []
    for level in range(2):
        at = lambda k: summed[16 * k + 8 * level : 16 * k + 8 * level + 8]
        solid = at(0)
        inverse = 1.0 / (1.0 + solid)
        covers.append((inverse, solid * inverse, [at(k) * inverse for k in range(1, 4)]))

    up, down = gz < 3, gz > 0
    right, left = lax.rem(gx + 1, 32), lax.rem(gx + 31, 32)

    def halo(step):
        def copy(k, src, dst, device):
            return pltpu.make_async_remote_copy(
                src_ref=src,
                dst_ref=dst,
                send_sem=h_send.at[step, k],
                recv_sem=h_recv.at[step, k],
                device_id=device,
                device_id_type=MESH,
            )

        both = [
            copy(0, edge_s.at[step, 0], edge_r.at[step, 0], (gz, right)),
            copy(1, edge_s.at[step, 1], edge_r.at[step, 1], (gz, left)),
        ]
        upward = [
            copy(2, corner_s.at[step, 0, 0], corner_r.at[step, 0, 0], (gz + 1, right)),
            copy(3, corner_s.at[step, 1, 0], corner_r.at[step, 1, 0], (gz + 1, left)),
            copy(4, post.at[step, pl.ds(18, 9), 1], z_r.at[step, 0], (gz + 1, gx)),
        ]
        downward = [
            copy(5, corner_s.at[step, 0, 1], corner_r.at[step, 0, 1], (gz - 1, right)),
            copy(6, corner_s.at[step, 1, 1], corner_r.at[step, 1, 1], (gz - 1, left)),
            copy(7, post.at[step, pl.ds(0, 9), 0], z_r.at[step, 1], (gz - 1, gx)),
        ]
        return both, upward, downward

    def edge_row(i, level):
        cz, _, cy = VEL[i]
        if cz == 0:
            return 3 * level + cy + 1
        return (6 if cz > 0 else 9) + cy + 1

    def is_corner(i, level):
        return (VEL[i][0] > 0 and level == 1) or (VEL[i][0] < 0 and level == 0)

    def send_halo(step):
        for i in range(27):
            cz, cx, cy = VEL[i]
            if cx == 0:
                continue
            side, row = (0, 7) if cx > 0 else (1, 0)
            for level in range(2):
                edge = post[step, i, level, row : row + 1, :]
                if is_corner(i, level):
                    corner_s[step, side, 0 if cz > 0 else 1, cy + 1 : cy + 2, :] = edge
                else:
                    k = edge_row(i, level)
                    edge_s[step, side, k : k + 1, :] = edge
        both, upward, downward = halo(step)

        @pl.when(up)
        def _():
            for c in upward:
                c.start()

        @pl.when(down)
        def _():
            for c in downward:
                c.start()

        for c in both:
            c.start()

    def wait_halo(step):
        both, upward, downward = halo(step)
        for c in both:
            c.wait_recv()

        @pl.when(down)
        def _():
            for c in upward:
                c.wait_recv()

        @pl.when(up)
        def _():
            for c in downward:
                c.wait_recv()

    sub = iota((8, 128), 0)

    def streamed(step, i, level):
        cz, cx, cy = VEL[i]
        origin = level - cz
        outside = origin < 0 or origin > 1
        if outside:
            z_side = 0 if cz > 0 else 1
            value = z_r[step, z_side, i - 18 if cz > 0 else i]
        else:
            value = post[step, i, origin]
        if cx:
            side = 0 if cx > 0 else 1
            if outside:
                row = corner_r[step, side, z_side, cy + 1 : cy + 2, :]
            else:
                k = edge_row(i, origin)
                row = edge_r[step, side, k : k + 1, :]
            value = pltpu.roll(value, cx % 8, 0)
            value = jnp.where(sub == (0 if cx > 0 else 7), jnp.broadcast_to(row, (8, 128)), value)
        if cy:
            value = pltpu.roll(value, cy % 128, 1)
        if outside:
            wall = gz == 0 if cz > 0 else gz == 3
            value = jnp.where(wall, post[step, 26 - i, level], value)
        return value

    for level in range(2):
        _, share, us = covers[level]
        finish(0, level, first[level][0], share, us)
    send_halo(0)
    wait_halo(0)

    second = []
    pushes = [[None, None] for _ in range(3)]
    for level in range(2):
        f = []
        for i in range(27):
            v = streamed(0, i, level)
            cells[i, level] = v
            f.append(v)
        rho, mom = moments(f)
        second.append((rho, mom))
        inverse, _, us = covers[level]
        rho_sum = first[level][0] + rho
        for k in range(3):
            pushes[k][level] = (us[k] * rho_sum - (first[level][1][k] + mom[k])) * inverse

    push = jnp.concatenate([pushes[k][level] for k in range(3) for level in range(2)], axis=0)
    high, low = split(-push)
    grains = recv_f[...].reshape(SLOTS, 128)
    all_lines = nt(high, grains) + nt(low, grains)
    match = match_s[...]
    diag = iota((CAP, SLOTS), 0) == iota((CAP, SLOTS), 1) % CAP
    parts = []
    for k in range(3):
        force = jnp.sum(match * all_lines[16 * k : 16 * k + 16], axis=0, keepdims=True)
        parts.append(jnp.where(diag, force, 0.0))
    parts.append(jnp.zeros((DEV - 3 * CAP, SLOTS), F32))
    high, low = split(jnp.concatenate(parts, axis=0))
    owner = one_hot(iota((DEV, SLOTS), 0) == iota((DEV, SLOTS), 1) // CAP)
    send_r[...] = (nt(owner, high) + nt(owner, low)).reshape(DEV, 1, 128)
    to_all(send_r, recv_r, 2)
    own_r = pltpu.make_async_copy(send_r.at[me], recv_r.at[me], own_sem.at[2])
    own_r.start()

    for level in range(2):
        f = [cells[i, level] for i in range(27)]
        rho, mom = second[level]
        collide(f, rho, mom, level)
        _, share, us = covers[level]
        finish(1, level, rho, share, us)
    send_halo(1)
    wait_halo(1)
    for level in range(2):
        for i in range(27):
            f_out[i, level] = streamed(1, i, level)

    wait_all(send_r, recv_r, a_recv.at[2])
    own_r.wait()
    table = recv_r[...].reshape(DEV, 128).T[0 : 3 * CAP]
    high, low = split(table)
    chosen_b = chosen_s[...]
    per_grain = nn(high, chosen_b) + nn(low, chosen_b)
    rank_mask = rank_s[...]
    for k in range(3):
        force_out[k : k + 1, :] = jnp.sum(
            rank_mask * per_grain[CAP * k : CAP * k + CAP], axis=0, keepdims=True
        )

    wait_all(send_m, recv_m, a_send.at[0])
    wait_all(send_f, recv_f, a_send.at[1])
    wait_all(send_r, recv_r, a_send.at[2])
    for step in range(2):
        both, upward, downward = halo(step)
        for c in both:
            c.wait_send()

        @pl.when(up)
        def _():
            for c in upward:
                c.wait_send()

        @pl.when(down)
        def _():
            for c in downward:
                c.wait_send()


def per_device(populations, rates, grain_fraction, grain_velocity, grain_dest, grain_line):
    hbm = pl.BlockSpec(memory_space=pl.ANY)
    vmem = pl.BlockSpec(memory_space=pltpu.VMEM)
    dma = pltpu.SemaphoreType.DMA
    block = (27, 2, 8, 128)
    cells, force = pl.pallas_call(
        kernel,
        out_shape=(
            jax.ShapeDtypeStruct(block, F32),
            jax.ShapeDtypeStruct((3, GRAINS), F32),
        ),
        in_specs=[hbm, pl.BlockSpec(memory_space=pltpu.SMEM), hbm, hbm, hbm, hbm],
        out_specs=(vmem, vmem),
        scratch_shapes=[
            pltpu.VMEM(block, F32),
            pltpu.VMEM((GRAINS, 128), BF16),
            pltpu.VMEM((3, GRAINS), BF16),
            pltpu.VMEM((1, GRAINS), jnp.int32),
            pltpu.VMEM((1, GRAINS), jnp.int32),
            pltpu.VMEM((DEV, CAP, 128), BF16),
            pltpu.VMEM((DEV, 1, 128), F32),
            pltpu.VMEM((DEV, CAP, 128), BF16),
            pltpu.VMEM((DEV, 1, 128), F32),
            pltpu.VMEM((DEV, 1, 128), F32),
            pltpu.VMEM((DEV, 1, 128), F32),
            pltpu.VMEM(block, F32),
            pltpu.VMEM(block, F32),
            pltpu.VMEM((2,) + block, F32),
            pltpu.VMEM((2, 2, 16, 128), F32),
            pltpu.VMEM((2, 2, 2, 8, 128), F32),
            pltpu.VMEM((2, 2, 16, 128), F32),
            pltpu.VMEM((2, 2, 2, 8, 128), F32),
            pltpu.VMEM((2, 2, 9, 8, 128), F32),
            pltpu.VMEM((DEV, GRAINS), BF16),
            pltpu.VMEM((CAP, GRAINS), F32),
            pltpu.VMEM((16, SLOTS), F32),
            pltpu.VMEM(block, F32),
            dma((5,)),
            dma((3,)),
            dma((3,)),
            dma((2, 8)),
            dma((2, 8)),
            dma((3,)),
        ],
        compiler_params=pltpu.CompilerParams(collective_id=0, has_side_effects=True),
        name="lattice",
    )(
        populations,
        rates,
        grain_fraction,
        grain_velocity,
        grain_dest.reshape(1, GRAINS),
        grain_line.reshape(1, GRAINS),
    )
    scale = np.array([1.0 / w for w in WEIGHT], np.float32)[:, None, None, None]
    return cells * jnp.asarray(scale), force


def solution(mesh):
    in_specs = (
        P(None, "gz", "gx", None),
        P(),
        P(("gz", "gx"), None),
        P(None, ("gz", "gx")),
        P(("gz", "gx"), None),
        P(("gz", "gx")),
    )
    out_specs = (P(None, "gz", "gx", None), P(None, ("gz", "gx")))
    return jax.shard_map(
        per_device, mesh=mesh, in_specs=in_specs, out_specs=out_specs, check_vma=False
    )
```

time: 139 us -> 34.1 us (0.25)
  the two profiles are of different devices: /device:TPU:0 before, /device:TPU:1 now
where the time goes in v1:
time: 34.1 us; the launch traced here: 33.9 us
  Pallas kernels  30.3 us (89%)
  other arithmetic  1.73 us (5%)
  local copies, waits for them, and re-layouts  1.25 us (4%)
  between operations  0.65 us (2%)
    pallas_call x1, Pallas kernels, per_device(): pl.pallas_call(kernel, out_shape=(jax.ShapeDtypeStruct(block, F32), jax.S...  30.3 us
    mul x1, other arithmetic, per_device(): return (cells * jnp.asarray(scale), force)  1.73 us
    unnamed x5, local copies, waits for them, and re-layouts  1.25 us

profile of v1, /device:TPU:1, one launch (start us, length us, event | category | flops | bytes accessed | tf_op | source)
XLA Modules:
  0.0 33.9 jit_solution(3983819077313260327)
XLA Ops:
  0.6 30.3 %lattice.1 = (f32[27,2,8,128]{3,2,1,0:T(8,128)}, f32[3,512]{1,0:T(4,128)}) custom-call(f32[27,2,8,128]{3,2,1,0:T(8,128)} %pop_in.1, f32[27]{0:T(128)} %rates.1, bf16[512,128]{1,0:T(8,128)(2,1)} %frac_in.1, bf16[3,512]{1,0:T(4,128)(2,1)} %vel_in.1, s32[1,512]{1,0:T(1,128)} %bitcast.2, s32[1,512]{1,0:T(1,128)} %bitcast.3), custom_call_target="tpu_custom_call" | custom-call | tf_op jit(solution)/shard_map/lattice/pallas_call | solution.py:446
  30.9 0.0 copy-start.1
  30.9 0.6 %copy-done.1 = f32[27]{0:T(128)S(1)} copy-done((f32[27]{0:T(128)S(1)}, f32[27]{0:T(128)}, u32[]{:S(2)}) %copy-start.1) | copy-done | bytes 132
  31.6 0.0 copy-start
  31.6 1.7 %broadcast_multiply_fusion = f32[27,2,8,128]{3,2,1,0:T(8,128)} fusion(f32[27,2,8,128]{3,2,1,0:T(8,128)} %get-tuple-element.4, f32[27]{0:T(128)S(1)} %copy-done.1), kind=kLoop, calls=%fused_computation | loop fusion | flops 55296 | bytes 442476 | tf_op jit(solution)/shard_map/mul | solution.py:496
  33.3 0.0 copy-done
  33.3 0.6 %copy.10 = f32[3,512]{1,0:T(4,128)} copy(f32[3,512]{1,0:T(4,128)S(1)} %copy-done) | data formatting | bytes 12288
Async XLA Ops:
  30.9 0.7 %copy-start.1 = (f32[27]{0:T(128)S(1)}, f32[27]{0:T(128)}, u32[]{:S(2)}) copy-start(f32[27]{0:T(128)} %constant.4) | copy-start | bytes 328
  31.6 1.7 %copy-start = (f32[3,512]{1,0:T(4,128)S(1)}, f32[3,512]{1,0:T(4,128)}, u32[]{:S(2)}) copy-start(f32[3,512]{1,0:T(4,128)} %get-tuple-element.9) | copy-start | bytes 18436

commit v2 on v1

--- a/solution.py
+++ b/solution.py
@@ -3,7 +3,6 @@
 
 import jax
 import jax.numpy as jnp
-import numpy as np
 from jax import lax
 from jax.experimental import pallas as pl
 from jax.experimental.pallas import tpu as pltpu
@@ -115,9 +114,9 @@
 
 
 def kernel(
-    pop_in, rates, frac_in, vel_in, dest_in, line_in,
+    pop_in, rates_in, frac_in, vel_in, dest_in, line_in,
     f_out, force_out,
-    pop, frac, vel, dest, line,
+    rates, pop, frac, vel, dest, line,
     send_f, send_m, recv_f, recv_m, send_r, recv_r,
     keep, mix, post, edge_s, corner_s, edge_r, corner_r, z_r,
     chosen_s, rank_s, match_s, cells,
@@ -139,7 +138,7 @@
     loads = [
         pltpu.make_async_copy(src, dst, in_sem.at[k])
         for k, (src, dst) in enumerate(
-            ((dest_in, dest), (line_in, line), (vel_in, vel), (frac_in, frac), (pop_in, pop))
+            ((dest_in, dest), (line_in, line), (vel_in, vel), (frac_in, frac), (pop_in, pop), (rates_in, rates))
         )
     ]
     for load in loads:
@@ -216,6 +215,7 @@
             post[step, i, level] = keep[i, level] + share * (mix[i, level] + equil[i])
 
     loads[4].wait()
+    loads[5].wait()
     first = []
     for level in range(2):
         f = [pop[i, level] for i in range(27)]
@@ -405,7 +405,7 @@
     wait_halo(1)
     for level in range(2):
         for i in range(27):
-            f_out[i, level] = streamed(1, i, level)
+            f_out[i, level] = streamed(1, i, level) * (1.0 / WEIGHT[i])
 
     wait_all(send_r, recv_r, a_recv.at[2])
     own_r.wait()
@@ -438,6 +438,17 @@
                 c.wait_send()
 
 
+def write_out(cells, force, cells_out, force_out, sem):
+    copies = [
+        pltpu.make_async_copy(cells, cells_out, sem.at[0]),
+        pltpu.make_async_copy(force, force_out, sem.at[1]),
+    ]
+    for c in copies:
+        c.start()
+    for c in copies:
+        c.wait()
+
+
 def per_device(populations, rates, grain_fraction, grain_velocity, grain_dest, grain_line):
     hbm = pl.BlockSpec(memory_space=pl.ANY)
     vmem = pl.BlockSpec(memory_space=pltpu.VMEM)
@@ -446,12 +457,13 @@
     cells, force = pl.pallas_call(
         kernel,
         out_shape=(
-            jax.ShapeDtypeStruct(block, F32),
-            jax.ShapeDtypeStruct((3, GRAINS), F32),
+            pltpu.VMEM(block, F32),
+            pltpu.VMEM((3, GRAINS), F32),
         ),
-        in_specs=[hbm, pl.BlockSpec(memory_space=pltpu.SMEM), hbm, hbm, hbm, hbm],
+        in_specs=[hbm] * 6,
         out_specs=(vmem, vmem),
         scratch_shapes=[
+            pltpu.SMEM((27,), F32),
             pltpu.VMEM(block, F32),
             pltpu.VMEM((GRAINS, 128), BF16),
             pltpu.VMEM((3, GRAINS), BF16),
@@ -475,7 +487,7 @@
             pltpu.VMEM((CAP, GRAINS), F32),
             pltpu.VMEM((16, SLOTS), F32),
             pltpu.VMEM(block, F32),
-            dma((5,)),
+            dma((6,)),
             dma((3,)),
             dma((3,)),
             dma((2, 8)),
@@ -492,8 +504,15 @@
         grain_dest.reshape(1, GRAINS),
         grain_line.reshape(1, GRAINS),
     )
-    scale = np.array([1.0 / w for w in WEIGHT], np.float32)[:, None, None, None]
-    return cells * jnp.asarray(scale), force
+    return pl.pallas_call(
+        write_out,
+        out_shape=(jax.ShapeDtypeStruct(block, F32), jax.ShapeDtypeStruct((3, GRAINS), F32)),
+        in_specs=[hbm, hbm],
+        out_specs=(hbm, hbm),
+        scratch_shapes=[dma((2,))],
+        compiler_params=pltpu.CompilerParams(vmem_limit_bytes=1 << 20),
+        name="write_out",
+    )(cells, force)
 
 
 def solution(mesh):

time: 34.1 us -> 30.4 us (0.89)
  other arithmetic: 1.73 us -> 0 us
  local copies, waits for them, and re-layouts: 1.25 us -> 0 us
  Pallas kernels: 30.3 us -> 29.7 us
    mul x1 -> x0, other arithmetic: 1.73 us -> none  [per_device(): return (cells * jnp.asarray(scale), force)]
    unnamed x5 -> x0, local copies, waits for them, and re-layouts: 1.25 us -> none
    pallas_call x1 -> x2, Pallas kernels: 30.3 us -> 29.7 us  [the longest x1 29 us: per_device(): pl.pallas_call(kernel, out_shape=(pltpu.VMEM(block, F32), pltpu.VMEM((3,...]
where the time goes in v2:
time: 30.4 us; the launch traced here: 30.3 us
  Pallas kernels  29.7 us (98%)
  between operations  0.64 us (2%)
    pallas_call x1, Pallas kernels, per_device(): pl.pallas_call(kernel, out_shape=(pltpu.VMEM(block, F32), pltpu.VMEM((3,...  29 us
    pallas_call x1, Pallas kernels, per_device(): pl.pallas_call(write_out, out_shape=(jax.ShapeDtypeStruct(block, F32), ja...  0.71 us

profile of v2, /device:TPU:1, one launch (start us, length us, event | category | flops | bytes accessed | tf_op | source)
XLA Modules:
  0.0 30.3 jit_solution(4688781404364402960)
XLA Ops:
  0.6 29.0 %lattice.1 = (f32[27,2,8,128]{3,2,1,0:T(8,128)S(1)}, f32[3,512]{1,0:T(4,128)S(1)}) custom-call(f32[27,2,8,128]{3,2,1,0:T(8,128)} %pop_in.1, f32[27]{0:T(128)} %rates_in.1, bf16[512,128]{1,0:T(8,128)(2,1)} %frac_in.1, bf16[3,512]{1,0:T(4,128)(2,1)} %vel_in.1, s32[1,512]{1,0:T(1,128)} %bitcast.2, s32[1,512]{1,0:T(1,128)} %bitcast.3), custom_call_target="tpu_custom_call" | custom-call | tf_op jit(solution)/shard_map/lattice/pallas_call | solution.py:457
  29.6 0.7 %write_out.1 = (f32[27,2,8,128]{3,2,1,0:T(8,128)}, f32[3,512]{1,0:T(4,128)}) custom-call(f32[27,2,8,128]{3,2,1,0:T(8,128)S(1)} %get-tuple-element.4.cells, f32[3,512]{1,0:T(4,128)S(1)} %get-tuple-element.5.force), custom_call_target="tpu_custom_call" | custom-call | tf_op jit(solution)/shard_map/write_out/pallas_call | solution.py:507

commit v3 on v2

v3 whole, which is shorter than its diff:
```python
import functools
import itertools

import jax
import jax.numpy as jnp
from jax import lax
from jax.experimental import pallas as pl
from jax.experimental.pallas import tpu as pltpu
from jax.sharding import PartitionSpec as P

MESH = pl.DeviceIdType.MESH
F32 = jnp.float32
BF16 = jnp.bfloat16
DEV = 128
CAP = 8
GRAINS = 512
SLOTS = DEV * CAP
VEL = [(i // 9 - 1, i // 3 % 3 - 1, i % 3 - 1) for i in range(27)]
WEIGHT = [(8.0 / 27, 2.0 / 27, 1.0 / 54, 1.0 / 216)[sum(map(abs, c))] for c in VEL]
NT = (((1,), (1,)), ((), ()))


def ring(v):
    return min(v, 4 - v)


OFFSETS = sorted(
    (o for o in itertools.product(range(4), range(4), range(4), range(2)) if any(o)),
    key=lambda o: -(0.75 * (ring(o[0]) + ring(o[1]) + ring(o[2])) + 0.5 * sum(v > 0 for v in o[:3]) + 0.2 * o[3]),
)


def iota(shape, dim, dtype=jnp.int32):
    out = lax.broadcasted_iota(jnp.int32, shape, dim)
    return out if dtype == jnp.int32 else out.astype(dtype)


def one_hot(mask):
    return jnp.where(mask, 1.0, 0.0).astype(BF16)


def split(x):
    high = x.astype(BF16)
    low = (x - high.astype(F32)).astype(BF16)
    return high, low


def nt(a, b):
    return lax.dot_general(a, b, NT, preferred_element_type=F32)


def nn(a, b):
    return jnp.dot(a, b, preferred_element_type=F32)


def along_axes(values, triple):
    for stride in (1, 3, 9):
        out = [None] * 27
        for base in range(27):
            if base // stride % 3 == 0:
                idx = (base, base + stride, base + 2 * stride)
                for k, v in zip(idx, triple(*(values[j] for j in idx))):
                    out[k] = v
        values = out
    return values


def to_moments(a, b, c):
    s = a + c
    return s + b, c - a, s


def from_moments(m0, m1, m2):
    h0, h1 = 0.5 * m2, 0.5 * m1
    return h0 - h1, m0 - m2, h0 + h1


def moments(f):
    plane = {}
    for i in range(27):
        if f[i] is not None:
            for key in [None] + [(k, VEL[i][k]) for k in range(3) if VEL[i][k]]:
                plane[key] = f[i] if key not in plane else plane[key] + f[i]

    def along(k):
        if (k, 1) not in plane:
            return -plane[(k, -1)] if (k, -1) in plane else jnp.zeros_like(plane[None])
        return plane[(k, 1)] - plane[(k, -1)] if (k, -1) in plane else plane[(k, 1)]

    return plane[None], [along(k) for k in range(3)]


def add_moments(a, b):
    return a[0] + b[0], [p + q for p, q in zip(a[1], b[1])]


def equilibrium(rho, v):
    t = [3.0 * q for q in v]
    base = rho * (1.0 - 1.5 * (v[0] * v[0] + v[1] * v[1] + v[2] * v[2]))
    half = 0.5 * rho
    out = [None] * 27
    for i in range(13):
        along = None
        c = VEL[26 - i]
        for k in range(3):
            if c[k]:
                term = t[k]
                if along is None:
                    along = term if c[k] > 0 else -term
                else:
                    along = along + term if c[k] > 0 else along - term
        even = base + half * (along * along)
        odd = rho * along
        out[26 - i] = WEIGHT[i] * (even + odd)
        out[i] = WEIGHT[i] * (even - odd)
    out[13] = WEIGHT[13] * base
    return out


def kernel(
    pop_in, rates_in, frac_in, vel_in, dest_in, line_in,
    f_out, force_out,
    rates, pop, frac, vel, dest, line,
    send_f, send_m, recv_f, recv_m, send_r, recv_r,
    keep, mix, post, edge_s, edge_r, z_s, z_r,
    chosen_s, rank_s, match_s, cells,
    in_sem, a_send, a_recv, h_send, h_recv,
):
    gz, gx = lax.axis_index("gz"), lax.axis_index("gx")
    me = gz * 32 + gx
    yy, zz, core = gx // 8, gx // 2 % 4, gx % 2
    at_x = [lax.rem(gz + a, 4) for a in range(4)]
    at_y = [lax.rem(yy + b, 4) * 8 for b in range(4)]
    at_z = [lax.rem(zz + c, 4) * 2 for c in range(4)]
    at_core = [core, 1 - core]

    def peer(o):
        return at_x[o[0]], at_y[o[1]] + (at_z[o[2]] + at_core[o[3]])

    barrier = pltpu.get_barrier_semaphore()
    for o in OFFSETS:
        pl.semaphore_signal(barrier, inc=1, device_id=peer(o), device_id_type=MESH)

    loads = [
        pltpu.make_async_copy(src, dst, in_sem.at[k])
        for k, (src, dst) in enumerate(
            (
                (dest_in, dest),
                (line_in, line),
                (vel_in, vel),
                (frac_in, frac),
                (pop_in, pop),
                (rates_in, rates),
            )
        )
    ]
    for load in loads:
        load.start()

    earlier = one_hot(iota((GRAINS, GRAINS), 0) < iota((GRAINS, GRAINS), 1))
    loads[0].wait()
    target = dest[...]
    chosen = iota((DEV, GRAINS), 0) == target
    chosen_b = one_hot(chosen)
    chosen_s[...] = chosen_b
    before = nn(chosen_b, earlier)
    rank = jnp.sum(jnp.where(chosen, before, 0.0), axis=0, keepdims=True)
    rank_mask = jnp.where(iota((CAP, GRAINS), 0, F32) == rank, 1.0, 0.0)
    rank_s[...] = rank_mask

    loads[1].wait()
    loads[2].wait()
    speed = vel[...].astype(F32)
    values = [line[...].astype(F32)] + [speed[k : k + 1] for k in range(3)]
    rows = [rank_mask * v for v in values] + [jnp.zeros((DEV - 4 * CAP, GRAINS), F32)]
    send_m[...] = nt(chosen_b, jnp.concatenate(rows, axis=0).astype(BF16))

    loads[3].wait()
    place = target.astype(F32) * CAP + rank
    fractions = frac[...]
    for j in range(8):
        pick = one_hot(iota((128, GRAINS), 0, F32) + 128.0 * j == place)
        send_f[16 * j : 16 * j + 16] = nn(pick, fractions).astype(BF16).reshape(16, CAP, 128)
    recv_m[pl.ds(me, 1), :] = send_m[pl.ds(me, 1), :]
    recv_f[me] = send_f[me]

    pl.semaphore_wait(barrier, DEV - 1)

    def to_peer(o, src, dst, k, wide):
        d = peer(o)
        p = d[0] * 32 + d[1]
        pltpu.make_async_remote_copy(
            src_ref=src.at[p] if wide else src.at[pl.ds(p, 1)],
            dst_ref=dst.at[me] if wide else dst.at[pl.ds(me, 1)],
            send_sem=a_send.at[k],
            recv_sem=a_recv.at[k],
            device_id=d,
            device_id_type=MESH,
        ).start()

    def wait_all(src, dst, sem):
        pltpu.make_async_copy(src.at[pl.ds(0, DEV - 1)], dst.at[pl.ds(0, DEV - 1)], sem).wait()

    for o in OFFSETS:
        to_peer(o, send_m, recv_m, 0, False)
        to_peer(o, send_f, recv_f, 1, True)

    def collide(f, rho, mom, level):
        inverse = 1.0 / rho
        equil = equilibrium(rho, [m * inverse for m in mom])
        departure = [f[i] - equil[i] for i in range(27)]
        projected = along_axes(departure, to_moments)
        fluid = along_axes([projected[a] * (-rates[a]) for a in range(27)], from_moments)
        for i in range(27):
            keep[i, level] = f[i] + fluid[i]
            mix[i, level] = departure[26 - i] - f[i] - fluid[i]

    loads[4].wait()
    loads[5].wait()
    first = []
    for level in range(2):
        f = [pop[i, level] for i in range(27)]
        rho, mom = moments(f)
        first.append((rho, mom))
        collide(f, rho, mom, level)

    wait_all(send_m, recv_m, a_recv.at[0])
    diag = iota((CAP, 128), 0) == iota((CAP, 128), 1) % CAP
    spread = jnp.concatenate(
        [
            jnp.where(diag, jnp.broadcast_to(recv_m[s : s + 1, :], (CAP, 128)), 0.0)
            for s in range(DEV)
        ],
        axis=0,
    ).astype(BF16)
    sel = one_hot(iota((CAP, 128), 0) == iota((CAP, 128), 1) // CAP)
    info = nt(sel, spread)
    match = jnp.where(iota((16, SLOTS), 0, F32) == info[0:1], 1.0, 0.0)
    match_s[...] = match
    weights = jnp.concatenate(
        [match] + [match * info[k : k + 1] for k in range(1, 4)], axis=0
    ).astype(BF16)

    wait_all(send_f, recv_f, a_recv.at[1])
    summed = nn(weights, recv_f[...].reshape(SLOTS, 128))
    covers = []
    for level in range(2):
        at = lambda k: summed[16 * k + 8 * level : 16 * k + 8 * level + 8]
        solid = at(0)
        inverse = 1.0 / (1.0 + solid)
        covers.append((inverse, solid * inverse, [at(k) * inverse for k in range(1, 4)]))

    up, down = gz < 3, gz > 0
    right, left = lax.rem(gx + 1, 32), lax.rem(gx + 31, 32)
    sub = iota((8, 128), 0)

    def halo(step):
        def copy(k, src, dst, device):
            return pltpu.make_async_remote_copy(
                src_ref=src,
                dst_ref=dst,
                send_sem=h_send.at[k],
                recv_sem=h_recv.at[step, k],
                device_id=device,
                device_id_type=MESH,
            )

        def edge(k, side, row, rows, device):
            at = (step, side, slice(None), pl.ds(row, rows))
            return copy(k, edge_s.at[at], edge_r.at[at], device)

        return (
            [edge(0, 0, 0, 4, (gz, right)), edge(0, 1, 0, 4, (gz, left))],
            [edge(1, 0, 4, 1, (gz + 1, right)), edge(1, 1, 4, 1, (gz + 1, left))],
            [edge(2, 0, 5, 1, (gz - 1, right)), edge(2, 1, 5, 1, (gz - 1, left))],
            [copy(3, z_s.at[step, 0], z_r.at[step, 0], (gz + 1, gx))],
            [copy(4, z_s.at[step, 1], z_r.at[step, 1], (gz - 1, gx))],
        )

    def wait_bytes(step, k, sem):
        if k < 3:
            at = (step, slice(None), slice(None), pl.ds(*((0, 4), (4, 1), (5, 1))[k]))
            src, dst = edge_s.at[at], edge_r.at[at]
        else:
            src, dst = z_s.at[step, k - 3], z_r.at[step, k - 3]
        pltpu.make_async_copy(src, dst, sem).wait()

    sends = (None, up, down, up, down)
    comes = (None, down, up, down, up)

    def guarded(test, run):
        if test is None:
            run()
        else:
            pl.when(test)(run)

    def start(copies, groups):
        for k in groups:
            guarded(sends[k], lambda k=k: [c.start() for c in copies[k]] and None)

    def arrive(step, groups):
        for k in groups:
            guarded(comes[k], lambda k=k: wait_bytes(step, k, h_recv.at[step, k]))

    def sent(step):
        for k in range(5):
            guarded(sends[k], lambda k=k: wait_bytes(step, k, h_send.at[k]))

    def edge_row(i, origin):
        cz = VEL[i][0]
        if cz == 0:
            return origin
        if cz > 0:
            return 2 if origin == 0 else 4
        return 3 if origin == 1 else 5

    def shifted(value, i):
        _, cx, cy = VEL[i]
        if cx:
            value = pltpu.roll(value, cx % 8, 0)
            value = jnp.where(sub == (0 if cx > 0 else 7), 0.0, value)
        if cy:
            value = pltpu.roll(value, cy % 128, 1)
        return value

    def leave(step, rhos):
        copies = halo(step)
        equils = [equilibrium(rhos[level], covers[level][2]) for level in range(2)]

        def finish(i, level):
            value = keep[i, level] + covers[level][1] * (mix[i, level] + equils[level][i])
            post[i, level] = value
            return value

        for i in range(27):
            cx, cy = VEL[i][1:]
            if cx:
                for level in range(2):
                    value = finish(i, level)
                    side, row = (0, 7) if cx > 0 else (1, 0)
                    k = edge_row(i, level)
                    edge_s[step, side, cy + 1, k : k + 1, :] = value[row : row + 1]
        start(copies, (1, 2, 0))
        for i in range(27):
            if VEL[i][1] == 0:
                for level in range(2):
                    finish(i, level)
        for i in range(9):
            z_s[step, 0, i] = shifted(post[18 + i, 1], 18 + i)
            z_s[step, 1, i] = shifted(post[i, 0], i)
        start(copies, (3, 4))

    def inside(out):
        for i in range(27):
            for level in range(2):
                if 0 <= level - VEL[i][0] <= 1:
                    out[i, level] = shifted(post[i, level - VEL[i][0]], i)

    def through_walls(step, out):
        for i in range(9):
            out[18 + i, 0] = jnp.where(gz == 0, post[8 - i, 0], z_r[step, 0, i])
            out[i, 1] = jnp.where(gz == 3, post[26 - i, 1], z_r[step, 1, i])

    def moved_edges(step):
        return [
            [
                edge_r[step, side, cy + 1]
                if cy == 0
                else pltpu.roll(edge_r[step, side, cy + 1], cy % 128, 1)
                for cy in (-1, 0, 1)
            ]
            for side in range(2)
        ]

    def edge_values(edges, level):
        for i in range(27):
            cz, cx, cy = VEL[i]
            if cx:
                side = 0 if cx > 0 else 1
                origin = level - cz
                if origin < 0 or origin > 1:
                    k, wall = (4, gz == 0) if cz > 0 else (5, gz == 3)
                else:
                    k, wall = edge_row(i, origin), None
                row = edges[side][cy + 1][k : k + 1]
                yield i, (0 if cx > 0 else 7), row, wall

    leave(0, [first[level][0] for level in range(2)])
    inside(cells)
    partial = []
    for level in range(2):
        f = [
            cells[i, level] if 0 <= level - VEL[i][0] <= 1 else None for i in range(27)
        ]
        partial.append(moments(f))
    arrive(0, (3, 4))
    through_walls(0, cells)
    for level in range(2):
        f = [
            None if 0 <= level - VEL[i][0] <= 1 else cells[i, level] for i in range(27)
        ]
        partial[level] = add_moments(partial[level], moments(f))
    arrive(0, (0, 1, 2))
    edges = moved_edges(0)
    fixes = []
    for level in range(2):
        f = {0: [None] * 27, 7: [None] * 27}
        for i, x, row, wall in edge_values(edges, level):
            if wall is not None:
                row = jnp.where(wall, 0.0, row)
            f[x][i] = jnp.broadcast_to(row, (8, 128))
        for x in (0, 7):
            rho, mom = moments(f[x])
            here = sub == x
            extra = (jnp.where(here, rho, 0.0), [jnp.where(here, m, 0.0) for m in mom])
            partial[level] = add_moments(partial[level], extra)
    second = partial
    pushes = [[None, None] for _ in range(3)]
    for level in range(2):
        rho, mom = second[level]
        inverse, _, us = covers[level]
        rho_sum = first[level][0] + rho
        for k in range(3):
            pushes[k][level] = ((first[level][1][k] + mom[k]) - us[k] * rho_sum) * inverse

    push = jnp.concatenate([pushes[k][level] for k in range(3) for level in range(2)], axis=0)
    high, low = split(push)
    grains = recv_f[...].reshape(SLOTS, 128)
    all_lines = nt(high, grains) + nt(low, grains)
    match = match_s[...]
    diag = iota((CAP, SLOTS), 0) == iota((CAP, SLOTS), 1) % CAP
    parts = []
    for k in range(3):
        force = jnp.sum(match * all_lines[16 * k : 16 * k + 16], axis=0, keepdims=True)
        parts.append(jnp.where(diag, force, 0.0))
    halves = split(jnp.concatenate(parts, axis=0))
    owner = one_hot(iota((DEV, SLOTS), 0) == iota((DEV, SLOTS), 1) // CAP)
    both = jnp.concatenate([h.astype(F32) for h in halves] + [jnp.zeros((DEV - 48, SLOTS), F32)], axis=0)
    send_r[...] = nt(owner, both.astype(BF16))
    recv_r[pl.ds(me, 1), :] = send_r[pl.ds(me, 1), :]
    for o in OFFSETS:
        to_peer(o, send_r, recv_r, 2, False)

    for level in range(2):
        for i, x, row, wall in edge_values(edges, level):
            if wall is not None:
                row = jnp.where(wall, cells[i, level, x : x + 1, :], row)
            cells[i, level, x : x + 1, :] = row
    for level in range(2):
        f = [cells[i, level] for i in range(27)]
        rho, mom = second[level]
        collide(f, rho, mom, level)
    sent(0)
    leave(1, [second[level][0] for level in range(2)])
    inside(f_out)
    arrive(1, (3, 4))
    through_walls(1, f_out)
    arrive(1, (0, 1, 2))
    edges = moved_edges(1)
    for level in range(2):
        for i, x, row, wall in edge_values(edges, level):
            if wall is not None:
                row = jnp.where(wall, f_out[i, level, x : x + 1, :], row)
            f_out[i, level, x : x + 1, :] = row
    for i in range(27):
        for level in range(2):
            f_out[i, level] = f_out[i, level] * (1.0 / WEIGHT[i])

    wait_all(send_r, recv_r, a_recv.at[2])
    table = recv_r[...].T[0 : 6 * CAP].astype(BF16)
    per_grain = nn(table, chosen_s[...])
    rank_mask = rank_s[...]
    for k in range(3):
        at = CAP * k
        total = per_grain[at : at + CAP] + per_grain[24 + at : 24 + at + CAP]
        force_out[k : k + 1, :] = jnp.sum(rank_mask * total, axis=0, keepdims=True)

    wait_all(send_m, recv_m, a_send.at[0])
    wait_all(send_f, recv_f, a_send.at[1])
    wait_all(send_r, recv_r, a_send.at[2])
    sent(1)


def write_out(cells, force, cells_out, force_out, sem):
    copies = [
        pltpu.make_async_copy(cells, cells_out, sem.at[0]),
        pltpu.make_async_copy(force, force_out, sem.at[1]),
    ]
    for c in copies:
        c.start()
    for c in copies:
        c.wait()


def per_device(populations, rates, grain_fraction, grain_velocity, grain_dest, grain_line):
    hbm = pl.BlockSpec(memory_space=pl.ANY)
    vmem = pl.BlockSpec(memory_space=pltpu.VMEM)
    dma = pltpu.SemaphoreType.DMA
    block = (27, 2, 8, 128)
    cells, force = pl.pallas_call(
        kernel,
        out_shape=(
            pltpu.VMEM(block, F32),
            pltpu.VMEM((3, GRAINS), F32),
        ),
        in_specs=[hbm] * 6,
        out_specs=(vmem, vmem),
        scratch_shapes=[
            pltpu.SMEM((27,), F32),
            pltpu.VMEM(block, F32),
            pltpu.VMEM((GRAINS, 128), BF16),
            pltpu.VMEM((3, GRAINS), BF16),
            pltpu.VMEM((1, GRAINS), jnp.int32),
            pltpu.VMEM((1, GRAINS), jnp.int32),
            pltpu.VMEM((DEV, CAP, 128), BF16),
            pltpu.VMEM((DEV, 128), F32),
            pltpu.VMEM((DEV, CAP, 128), BF16),
            pltpu.VMEM((DEV, 128), F32),
            pltpu.VMEM((DEV, 128), F32),
            pltpu.VMEM((DEV, 128), F32),
            pltpu.VMEM(block, F32),
            pltpu.VMEM(block, F32),
            pltpu.VMEM(block, F32),
            pltpu.VMEM((2, 2, 3, 8, 128), F32),
            pltpu.VMEM((2, 2, 3, 8, 128), F32),
            pltpu.VMEM((2, 2, 9, 8, 128), F32),
            pltpu.VMEM((2, 2, 9, 8, 128), F32),
            pltpu.VMEM((DEV, GRAINS), BF16),
            pltpu.VMEM((CAP, GRAINS), F32),
            pltpu.VMEM((16, SLOTS), F32),
            pltpu.VMEM(block, F32),
            dma((6,)),
            dma((3,)),
            dma((3,)),
            dma((5,)),
            dma((2, 5)),
        ],
        compiler_params=pltpu.CompilerParams(collective_id=0, has_side_effects=True),
        name="lattice",
    )(
        populations,
        rates,
        grain_fraction,
        grain_velocity,
        grain_dest.reshape(1, GRAINS),
        grain_line.reshape(1, GRAINS),
    )
    return pl.pallas_call(
        write_out,
        out_shape=(jax.ShapeDtypeStruct(block, F32), jax.ShapeDtypeStruct((3, GRAINS), F32)),
        in_specs=[hbm, hbm],
        out_specs=(hbm, hbm),
        scratch_shapes=[dma((2,))],
        compiler_params=pltpu.CompilerParams(vmem_limit_bytes=1 << 20),
        name="write_out",
    )(cells, force)


def solution(mesh):
    in_specs = (
        P(None, "gz", "gx", None),
        P(),
        P(("gz", "gx"), None),
        P(None, ("gz", "gx")),
        P(("gz", "gx"), None),
        P(("gz", "gx")),
    )
    out_specs = (P(None, "gz", "gx", None), P(None, ("gz", "gx")))
    return jax.shard_map(
        per_device, mesh=mesh, in_specs=in_specs, out_specs=out_specs, check_vma=False
    )
```

time: 30.4 us -> 29.5 us (0.970)
  Pallas kernels: 29.7 us -> 28.8 us
    pallas_call x1, Pallas kernels: 29 us -> 28.1 us  [per_device(): pl.pallas_call(kernel, out_shape=(pltpu.VMEM(block, F32), pltpu.VMEM((3,...]
where the time goes in v3:
time: 29.5 us; the launch traced here: 29.4 us
  Pallas kernels  28.8 us (98%)
  between operations  0.64 us (2%)
    pallas_call x1, Pallas kernels, per_device(): pl.pallas_call(kernel, out_shape=(pltpu.VMEM(block, F32), pltpu.VMEM((3,...  28.1 us
    pallas_call x1, Pallas kernels, per_device(): pl.pallas_call(write_out, out_shape=(jax.ShapeDtypeStruct(block, F32), ja...  0.71 us

profile of v3, /device:TPU:1, one launch (start us, length us, event | category | flops | bytes accessed | tf_op | source)
XLA Modules:
  0.0 29.4 jit_solution(12811816371746454465)
XLA Ops:
  0.6 28.1 %lattice.1 = (f32[27,2,8,128]{3,2,1,0:T(8,128)S(1)}, f32[3,512]{1,0:T(4,128)S(1)}) custom-call(f32[27,2,8,128]{3,2,1,0:T(8,128)} %pop_in.1, f32[27]{0:T(128)} %rates_in.1, bf16[512,128]{1,0:T(8,128)(2,1)} %frac_in.1, bf16[3,512]{1,0:T(4,128)(2,1)} %vel_in.1, s32[1,512]{1,0:T(1,128)} %bitcast.2, s32[1,512]{1,0:T(1,128)} %bitcast.3), custom_call_target="tpu_custom_call" | custom-call | tf_op jit(solution)/shard_map/lattice/pallas_call | solution.py:500
  28.7 0.7 %write_out.1 = (f32[27,2,8,128]{3,2,1,0:T(8,128)}, f32[3,512]{1,0:T(4,128)}) custom-call(f32[27,2,8,128]{3,2,1,0:T(8,128)S(1)} %get-tuple-element.4.cells, f32[3,512]{1,0:T(4,128)S(1)} %get-tuple-element.5.force), custom_call_target="tpu_custom_call" | custom-call | tf_op jit(solution)/shard_map/write_out/pallas_call | solution.py:548

commit v4 on v3

--- a/solution.py
+++ b/solution.py
@@ -119,12 +119,12 @@
 
 def kernel(
     pop_in, rates_in, frac_in, vel_in, dest_in, line_in,
-    f_out, force_out,
+    f_out, table_out, chosen_s, rank_s,
     rates, pop, frac, vel, dest, line,
     send_f, send_m, recv_f, recv_m, send_r, recv_r,
     keep, mix, post, edge_s, edge_r, z_s, z_r,
-    chosen_s, rank_s, match_s, cells,
-    in_sem, a_send, a_recv, h_send, h_recv,
+    match_s, cells,
+    a_send, a_recv, h_send, h_recv,
 ):
     gz, gx = lax.axis_index("gz"), lax.axis_index("gx")
     me = gz * 32 + gx
@@ -142,16 +142,14 @@
         pl.semaphore_signal(barrier, inc=1, device_id=peer(o), device_id_type=MESH)
 
     loads = [
-        pltpu.make_async_copy(src, dst, in_sem.at[k])
-        for k, (src, dst) in enumerate(
-            (
-                (dest_in, dest),
-                (line_in, line),
-                (vel_in, vel),
-                (frac_in, frac),
-                (pop_in, pop),
-                (rates_in, rates),
-            )
+        pltpu.make_async_copy(src, dst, sem)
+        for src, dst, sem in (
+            (dest_in, dest, h_send.at[0]),
+            (line_in, line, h_send.at[1]),
+            (vel_in, vel, h_send.at[2]),
+            (frac_in, frac, a_send.at[1]),
+            (pop_in, pop, h_send.at[3]),
+            (rates_in, rates, h_send.at[4]),
         )
     ]
     for load in loads:
@@ -423,6 +421,16 @@
         for k in range(3):
             pushes[k][level] = ((first[level][1][k] + mom[k]) - us[k] * rho_sum) * inverse
 
+    for level in range(1):
+        for i, x, row, wall in edge_values(edges, level):
+            if wall is not None:
+                row = jnp.where(wall, cells[i, level, x : x + 1, :], row)
+            cells[i, level, x : x + 1, :] = row
+    for level in range(1):
+        f = [cells[i, level] for i in range(27)]
+        rho, mom = second[level]
+        collide(f, rho, mom, level)
+
     push = jnp.concatenate([pushes[k][level] for k in range(3) for level in range(2)], axis=0)
     high, low = split(push)
     grains = recv_f[...].reshape(SLOTS, 128)
@@ -441,12 +449,12 @@
     for o in OFFSETS:
         to_peer(o, send_r, recv_r, 2, False)
 
-    for level in range(2):
+    for level in range(1, 2):
         for i, x, row, wall in edge_values(edges, level):
             if wall is not None:
                 row = jnp.where(wall, cells[i, level, x : x + 1, :], row)
             cells[i, level, x : x + 1, :] = row
-    for level in range(2):
+    for level in range(1, 2):
         f = [cells[i, level] for i in range(27)]
         rho, mom = second[level]
         collide(f, rho, mom, level)
@@ -467,13 +475,7 @@
             f_out[i, level] = f_out[i, level] * (1.0 / WEIGHT[i])
 
     wait_all(send_r, recv_r, a_recv.at[2])
-    table = recv_r[...].T[0 : 6 * CAP].astype(BF16)
-    per_grain = nn(table, chosen_s[...])
-    rank_mask = rank_s[...]
-    for k in range(3):
-        at = CAP * k
-        total = per_grain[at : at + CAP] + per_grain[24 + at : 24 + at + CAP]
-        force_out[k : k + 1, :] = jnp.sum(rank_mask * total, axis=0, keepdims=True)
+    table_out[...] = recv_r[...]
 
     wait_all(send_m, recv_m, a_send.at[0])
     wait_all(send_f, recv_f, a_send.at[1])
@@ -481,15 +483,20 @@
     sent(1)
 
 
-def write_out(cells, force, cells_out, force_out, sem):
-    copies = [
-        pltpu.make_async_copy(cells, cells_out, sem.at[0]),
-        pltpu.make_async_copy(force, force_out, sem.at[1]),
-    ]
-    for c in copies:
-        c.start()
-    for c in copies:
-        c.wait()
+def write_out(cells, table_in, chosen_in, rank_in, cells_out, force_out, force, sem):
+    first = pltpu.make_async_copy(cells, cells_out, sem.at[0])
+    first.start()
+    table = table_in[...].T[0 : 6 * CAP].astype(BF16)
+    per_grain = nn(table, chosen_in[...])
+    rank_mask = rank_in[...]
+    for k in range(3):
+        at = CAP * k
+        total = per_grain[at : at + CAP] + per_grain[24 + at : 24 + at + CAP]
+        force[k : k + 1, :] = jnp.sum(rank_mask * total, axis=0, keepdims=True)
+    second = pltpu.make_async_copy(force, force_out, sem.at[1])
+    second.start()
+    first.wait()
+    second.wait()
 
 
 def per_device(populations, rates, grain_fraction, grain_velocity, grain_dest, grain_line):
@@ -497,14 +504,16 @@
     vmem = pl.BlockSpec(memory_space=pltpu.VMEM)
     dma = pltpu.SemaphoreType.DMA
     block = (27, 2, 8, 128)
-    cells, force = pl.pallas_call(
+    parts = pl.pallas_call(
         kernel,
         out_shape=(
             pltpu.VMEM(block, F32),
-            pltpu.VMEM((3, GRAINS), F32),
+            pltpu.VMEM((DEV, 128), F32),
+            pltpu.VMEM((DEV, GRAINS), BF16),
+            pltpu.VMEM((CAP, GRAINS), F32),
         ),
         in_specs=[hbm] * 6,
-        out_specs=(vmem, vmem),
+        out_specs=(vmem,) * 4,
         scratch_shapes=[
             pltpu.SMEM((27,), F32),
             pltpu.VMEM(block, F32),
@@ -525,11 +534,8 @@
             pltpu.VMEM((2, 2, 3, 8, 128), F32),
             pltpu.VMEM((2, 2, 9, 8, 128), F32),
             pltpu.VMEM((2, 2, 9, 8, 128), F32),
-            pltpu.VMEM((DEV, GRAINS), BF16),
-            pltpu.VMEM((CAP, GRAINS), F32),
             pltpu.VMEM((16, SLOTS), F32),
             pltpu.VMEM(block, F32),
-            dma((6,)),
             dma((3,)),
             dma((3,)),
             dma((5,)),
@@ -548,12 +554,12 @@
     return pl.pallas_call(
         write_out,
         out_shape=(jax.ShapeDtypeStruct(block, F32), jax.ShapeDtypeStruct((3, GRAINS), F32)),
-        in_specs=[hbm, hbm],
+        in_specs=[hbm, vmem, vmem, vmem],
         out_specs=(hbm, hbm),
-        scratch_shapes=[dma((2,))],
+        scratch_shapes=[pltpu.VMEM((3, GRAINS), F32), dma((2,))],
         compiler_params=pltpu.CompilerParams(vmem_limit_bytes=1 << 20),
         name="write_out",
-    )(cells, force)
+    )(*parts)
 
 
 def solution(mesh):

time: 29.5 us -> 29.4 us (level)
  no operation moved by 1% of the time
where the time goes in v4:
time: 29.4 us; the launch traced here: 29.3 us
  Pallas kernels  28.7 us (98%)
  between operations  0.64 us (2%)
    pallas_call x1, Pallas kernels, per_device(): pl.pallas_call(kernel, out_shape=(pltpu.VMEM(block, F32), pltpu.VMEM((DEV...  27.9 us
    pallas_call x1, Pallas kernels, per_device(): pl.pallas_call(write_out, out_shape=(jax.ShapeDtypeStruct(block, F32), ja...  0.83 us

profile of v4, /device:TPU:1, one launch (start us, length us, event | category | flops | bytes accessed | tf_op | source)
XLA Modules:
  0.0 29.3 jit_solution(11620053185866706404)
XLA Ops:
  0.6 27.9 %lattice.1 = (f32[27,2,8,128]{3,2,1,0:T(8,128)S(1)}, f32[128,128]{1,0:T(8,128)S(1)}, bf16[128,512]{1,0:T(8,128)(2,1)S(1)}, f32[8,512]{1,0:T(8,128)S(1)}) custom-call(f32[27,2,8,128]{3,2,1,0:T(8,128)} %pop_in.1, f32[27]{0:T(128)} %rates_in.1, bf16[512,128]{1,0:T(8,128)(2,1)} %frac_in.1, bf16[3,512]{1,0:T(4,128)(2,1)} %vel_in.1, s32[1,512]{1,0:T(1,128)} %bitcast.2, ...), custom_call_target="tpu_custom_call" | custom-call | tf_op jit(solution)/shard_map/lattice/pallas_call | solution.py:507
  28.5 0.8 %write_out.1 = (f32[27,2,8,128]{3,2,1,0:T(8,128)}, f32[3,512]{1,0:T(4,128)}) custom-call(f32[27,2,8,128]{3,2,1,0:T(8,128)S(1)} %get-tuple-element.6.cells, f32[128,128]{1,0:T(8,128)S(1)} %get-tuple-element.7.table_in, bf16[128,512]{1,0:T(8,128)(2,1)S(1)} %get-tuple-element.8.chosen_in, f32[8,512]{1,0:T(8,128)S(1)} %get-tuple-element.9.rank_in), custom_call_target="tpu_custom_call" | custom-call | tf_op jit(solution)/shard_map/write_out/pallas_call | solution.py:554

commit v5 on v4

--- a/solution.py
+++ b/solution.py
@@ -28,6 +28,9 @@
     (o for o in itertools.product(range(4), range(4), range(4), range(2)) if any(o)),
     key=lambda o: -(0.75 * (ring(o[0]) + ring(o[1]) + ring(o[2])) + 0.5 * sum(v > 0 for v in o[:3]) + 0.2 * o[3]),
 )
+
+
+LEAD = 32
 
 
 def iota(shape, dim, dtype=jnp.int32):
@@ -199,9 +202,11 @@
     def wait_all(src, dst, sem):
         pltpu.make_async_copy(src.at[pl.ds(0, DEV - 1)], dst.at[pl.ds(0, DEV - 1)], sem).wait()
 
-    for o in OFFSETS:
-        to_peer(o, send_m, recv_m, 0, False)
-        to_peer(o, send_f, recv_f, 1, True)
+    for k in range(DEV - 1 + LEAD):
+        if k < DEV - 1:
+            to_peer(OFFSETS[k], send_m, recv_m, 0, False)
+        if k >= LEAD:
+            to_peer(OFFSETS[k - LEAD], send_f, recv_f, 1, True)
 
     def collide(f, rho, mom, level):
         inverse = 1.0 / rho
@@ -421,15 +426,6 @@
         for k in range(3):
             pushes[k][level] = ((first[level][1][k] + mom[k]) - us[k] * rho_sum) * inverse
 
-    for level in range(1):
-        for i, x, row, wall in edge_values(edges, level):
-            if wall is not None:
-                row = jnp.where(wall, cells[i, level, x : x + 1, :], row)
-            cells[i, level, x : x + 1, :] = row
-    for level in range(1):
-        f = [cells[i, level] for i in range(27)]
-        rho, mom = second[level]
-        collide(f, rho, mom, level)
 
     push = jnp.concatenate([pushes[k][level] for k in range(3) for level in range(2)], axis=0)
     high, low = split(push)
@@ -449,12 +445,12 @@
     for o in OFFSETS:
         to_peer(o, send_r, recv_r, 2, False)
 
-    for level in range(1, 2):
+    for level in range(2):
         for i, x, row, wall in edge_values(edges, level):
             if wall is not None:
                 row = jnp.where(wall, cells[i, level, x : x + 1, :], row)
             cells[i, level, x : x + 1, :] = row
-    for level in range(1, 2):
+    for level in range(2):
         f = [cells[i, level] for i in range(27)]
         rho, mom = second[level]
         collide(f, rho, mom, level)

time: 29.4 us -> 29.3 us (level)
  no operation moved by 1% of the time
where the time goes in v5:
time: 29.3 us; the launch traced here: 29.2 us
  Pallas kernels  28.5 us (97%)
  between operations  0.64 us (2%)
    pallas_call x1, Pallas kernels, per_device(): pl.pallas_call(kernel, out_shape=(pltpu.VMEM(block, F32), pltpu.VMEM((DEV...  27.7 us
    pallas_call x1, Pallas kernels, per_device(): pl.pallas_call(write_out, out_shape=(jax.ShapeDtypeStruct(block, F32), ja...  0.83 us

profile of v5, /device:TPU:1, one launch (start us, length us, event | category | flops | bytes accessed | tf_op | source)
XLA Modules:
  0.0 29.2 jit_solution(5232376136867542839)
XLA Ops:
  0.6 27.7 %lattice.1 = (f32[27,2,8,128]{3,2,1,0:T(8,128)S(1)}, f32[128,128]{1,0:T(8,128)S(1)}, bf16[128,512]{1,0:T(8,128)(2,1)S(1)}, f32[8,512]{1,0:T(8,128)S(1)}) custom-call(f32[27,2,8,128]{3,2,1,0:T(8,128)} %pop_in.1, f32[27]{0:T(128)} %rates_in.1, bf16[512,128]{1,0:T(8,128)(2,1)} %frac_in.1, bf16[3,512]{1,0:T(4,128)(2,1)} %vel_in.1, s32[1,512]{1,0:T(1,128)} %bitcast.2, ...), custom_call_target="tpu_custom_call" | custom-call | tf_op jit(solution)/shard_map/lattice/pallas_call | solution.py:503
  28.3 0.8 %write_out.1 = (f32[27,2,8,128]{3,2,1,0:T(8,128)}, f32[3,512]{1,0:T(4,128)}) custom-call(f32[27,2,8,128]{3,2,1,0:T(8,128)S(1)} %get-tuple-element.6.cells, f32[128,128]{1,0:T(8,128)S(1)} %get-tuple-element.7.table_in, bf16[128,512]{1,0:T(8,128)(2,1)S(1)} %get-tuple-element.8.chosen_in, f32[8,512]{1,0:T(8,128)S(1)} %get-tuple-element.9.rank_in), custom_call_target="tpu_custom_call" | custom-call | tf_op jit(solution)/shard_map/write_out/pallas_call | solution.py:550

commit v6 on v5

--- a/solution.py
+++ b/solution.py
@@ -470,13 +470,12 @@
         for level in range(2):
             f_out[i, level] = f_out[i, level] * (1.0 / WEIGHT[i])
 
+    wait_all(send_m, recv_m, a_send.at[0])
+    wait_all(send_f, recv_f, a_send.at[1])
+    sent(1)
+    wait_all(send_r, recv_r, a_send.at[2])
     wait_all(send_r, recv_r, a_recv.at[2])
     table_out[...] = recv_r[...]
-
-    wait_all(send_m, recv_m, a_send.at[0])
-    wait_all(send_f, recv_f, a_send.at[1])
-    wait_all(send_r, recv_r, a_send.at[2])
-    sent(1)
 
 
 def write_out(cells, table_in, chosen_in, rank_in, cells_out, force_out, force, sem):

time: 29.3 us -> 29.3 us (level)
  no operation moved by 1% of the time
where the time goes in v6:
time: 29.3 us; the launch traced here: 29.1 us
  Pallas kernels  28.5 us (97%)
  between operations  0.64 us (2%)
    pallas_call x1, Pallas kernels, per_device(): pl.pallas_call(kernel, out_shape=(pltpu.VMEM(block, F32), pltpu.VMEM((DEV...  27.7 us
    pallas_call x1, Pallas kernels, per_device(): pl.pallas_call(write_out, out_shape=(jax.ShapeDtypeStruct(block, F32), ja...  0.83 us

profile of v6, /device:TPU:1, one launch (start us, length us, event | category | flops | bytes accessed | tf_op | source)
XLA Modules:
  0.0 29.1 jit_solution(16531865450076529304)
XLA Ops:
  0.6 27.7 %lattice.1 = (f32[27,2,8,128]{3,2,1,0:T(8,128)S(1)}, f32[128,128]{1,0:T(8,128)S(1)}, bf16[128,512]{1,0:T(8,128)(2,1)S(1)}, f32[8,512]{1,0:T(8,128)S(1)}) custom-call(f32[27,2,8,128]{3,2,1,0:T(8,128)} %pop_in.1, f32[27]{0:T(128)} %rates_in.1, bf16[512,128]{1,0:T(8,128)(2,1)} %frac_in.1, bf16[3,512]{1,0:T(4,128)(2,1)} %vel_in.1, s32[1,512]{1,0:T(1,128)} %bitcast.2, ...), custom_call_target="tpu_custom_call" | custom-call | tf_op jit(solution)/shard_map/lattice/pallas_call | solution.py:502
  28.3 0.8 %write_out.1 = (f32[27,2,8,128]{3,2,1,0:T(8,128)}, f32[3,512]{1,0:T(4,128)}) custom-call(f32[27,2,8,128]{3,2,1,0:T(8,128)S(1)} %get-tuple-element.6.cells, f32[128,128]{1,0:T(8,128)S(1)} %get-tuple-element.7.table_in, bf16[128,512]{1,0:T(8,128)(2,1)S(1)} %get-tuple-element.8.chosen_in, f32[8,512]{1,0:T(8,128)S(1)} %get-tuple-element.9.rank_in), custom_call_target="tpu_custom_call" | custom-call | tf_op jit(solution)/shard_map/write_out/pallas_call | solution.py:549
